TPU v7x, 256 devices: a whole 4x4x8 slice. The times are simulated.
256 devices in a mesh: context: 32 (over z, x_lo, core), tensor: 8 (over x_hi, y).
Axes of the slice: x: 4 (x_hi: 2, x_lo: 2; x = x_hi * 2 + x_lo), y: 4, z: 8, core: 2. Of those that a mesh axis runs over, the one named last changes fastest.
Arguments:
- activations: bfloat16 [6144, 5120], P(('context', 'tensor')), may hold values from -6 to 6
- queries: bfloat16 [6144, 5120], P('context', 'tensor'), may hold values from -44 to 44
- key_weight: bfloat16 [5120, 1024], P(None, 'tensor'), may hold values from -0.5 to 1.1
- value_projection_weight: bfloat16 [5120, 1024], P(None, 'tensor'), may hold values from -0.078125 to 0.078125
- output_gradient: bfloat16 [6144, 5120], P('context', 'tensor'), may hold values from -6 to 6
- span_order: int32 [64], replicated, may hold values from 0 to 63, as said below
- doc_ids: int32 [6144], replicated, may hold values from 0 to 4, as said below
Outputs:
- attended: bfloat16 [6144, 5120], P('context', 'tensor')
- grad_queries: bfloat16 [6144, 5120], P('context', 'tensor')
- grad_inputs: bfloat16 [6144, 5120], P(('context', 'tensor'))
- grad_key_weight: float32 [5120, 1024], P('context', 'tensor')
- grad_value_weight: float32 [5120, 1024], P('context', 'tensor')
Inputs may be any that keep to these rules, and one draw needn't show every extreme that they name: `span_order`: each number once. `doc_ids`: taken in order of positions, the document numbers never fall; one document holds exactly 3072 positions and none holds more.
All inputs are finite; a program needn't handle non-finite values.
Results may differ from a plain program's by a relative error of at most 0.02.
Values may be sent and summed in bfloat16 or wider, within the bound.
No kernel may reach another device: no remote copies, remote signals or barrier semaphores. Data moves between devices by JAX's collectives and lax.ppermute only.
A program may use at most 192 MiB of HBM per device.

v0:
```python
import functools
import math

import jax
import jax.numpy as jnp
from jax import lax
from jax.experimental import pallas as pl
from jax.experimental.pallas import tpu as pltpu
from jax.sharding import Mesh, PartitionSpec as P


HEAD = 128
SPAN = 96
GROUP = 4
BLOCK = GROUP * SPAN
CTX = ("z", "xl", "c")
TEN = ("xh", "y")
MASKED = -1e30


def brought(n_z):
    far = n_z // 2
    steps = [0] + [s * k for k in range(1, far) for s in (1, -1)]
    return [(k, side) for k in steps for side in (0, 1)] + [(far, 0), (far, 1)]


def attention_kernel(n_blocks, table_ref, limit_ref, q_ref, g_ref, *refs):
    blocks, refs = refs[:n_blocks], refs[n_blocks:]
    att_ref, gq_ref = refs[:2]
    outs, (kv_s, acc_s, s_s, qs, gs, o_s) = refs[2:8], refs[8:]
    halves = q_ref.shape[0] // SPAN
    n_spans = sum(out.shape[0] for out in outs)
    heads = q_ref.shape[1] // HEAD
    rows = heads * SPAN
    wide = qs.shape[0]
    inv_root = 1.0 / math.sqrt(HEAD)
    scale2 = inv_root * math.log2(math.e)

    def span_at(entry):
        return pl.ds(pl.multiple_of(table_ref[entry] * SPAN, SPAN), SPAN)

    entry = 0
    for ref in blocks:
        for j in range(ref.shape[0]):
            for i in range(halves):
                kv_s[span_at(entry), :] = ref[j, i * SPAN : (i + 1) * SPAN]
                entry += 1

    def clear(p, carry):
        acc_s[pl.ds(pl.multiple_of(p * SPAN, SPAN), SPAN), :] = jnp.zeros(
            (SPAN, 2 * HEAD), jnp.float32
        )
        return carry

    lax.fori_loop(0, n_spans, clear, 0)
    qs[rows:, :] = jnp.zeros((wide - rows, HEAD), qs.dtype)
    gs[rows:, :] = jnp.zeros((wide - rows, HEAD), gs.dtype)

    def one_span(i, done):
        own = pl.ds(pl.multiple_of(i * SPAN, SPAN), SPAN)
        for h in range(heads):
            qs[h * SPAN : (h + 1) * SPAN, :] = q_ref[own, h * HEAD : (h + 1) * HEAD]
            gs[h * SPAN : (h + 1) * SPAN, :] = g_ref[own, h * HEAD : (h + 1) * HEAD]
        lo, full_lo, full_hi, hi = (table_ref[2 * n_spans + 4 * i + j] for j in range(4))
        first, last = limit_ref[i, 0], limit_ref[i, 1]

        def block(b):
            return pl.ds(pl.multiple_of(b * BLOCK, BLOCK), BLOCK)

        def score(masked, b, top):
            s = lax.dot_general(
                kv_s[block(b), :HEAD], qs[...], (((1,), (1,)), ((), ())),
                preferred_element_type=jnp.float32,
            ) * scale2
            if masked:
                pos = lax.broadcasted_iota(jnp.int32, s.shape, 0) + b * BLOCK
                s = jnp.where((pos >= first) & (pos <= last), s, MASKED)
            s_s[block(b), :] = s
            return jnp.maximum(top, jnp.max(s.reshape(BLOCK // 8, 8, wide), axis=0))

        masked, plain = (functools.partial(score, m) for m in (True, False))
        top = jnp.full((8, wide), MASKED, jnp.float32)
        top = lax.fori_loop(lo, full_lo, masked, top)
        top = lax.fori_loop(full_lo, full_hi, plain, top)
        top = lax.fori_loop(full_hi, hi, masked, top)
        top = jnp.max(top, axis=0, keepdims=True)
        o_s[...] = jnp.zeros_like(o_s)

        def weigh(b, total):
            e = jnp.exp2(s_s[block(b), :] - top)
            s_s[block(b), :] = e
            o_s[...] += lax.dot_general(
                kv_s[block(b), HEAD:], e.astype(jnp.bfloat16), (((0,), (0,)), ((), ())),
                preferred_element_type=jnp.float32,
            )
            return total + jnp.sum(e.reshape(BLOCK // 8, 8, wide), axis=0)

        total = lax.fori_loop(lo, hi, weigh, jnp.zeros((8, wide), jnp.float32))
        share = 1.0 / jnp.sum(total, axis=0, keepdims=True)
        att = (o_s[...] * share).astype(jnp.bfloat16).astype(jnp.float32)
        delta = jnp.sum(att * gs[...].astype(jnp.float32).T, axis=0, keepdims=True)
        att = att.T.astype(jnp.bfloat16)
        for h in range(heads):
            att_ref[own, h * HEAD : (h + 1) * HEAD] = att[h * SPAN : (h + 1) * SPAN]
        o_s[...] = jnp.zeros_like(o_s)

        def back(b, carry):
            k = kv_s[block(b), :HEAD]
            v = kv_s[block(b), HEAD:]
            p = s_s[block(b), :] * share
            grad_p = lax.dot_general(
                v, gs[...], (((1,), (1,)), ((), ())), preferred_element_type=jnp.float32
            )
            grad_s = (p * (grad_p - delta) * inv_root).astype(jnp.bfloat16)
            acc_s[block(b), HEAD:] += jnp.dot(
                p.astype(jnp.bfloat16), gs[...], preferred_element_type=jnp.float32
            )
            acc_s[block(b), :HEAD] += jnp.dot(
                grad_s, qs[...], preferred_element_type=jnp.float32
            )
            o_s[...] += lax.dot_general(
                k, grad_s, (((0,), (0,)), ((), ())), preferred_element_type=jnp.float32
            )
            return carry

        lax.fori_loop(lo, hi, back, 0)
        grad_q = o_s[...].T.astype(jnp.bfloat16)
        for h in range(heads):
            gq_ref[own, h * HEAD : (h + 1) * HEAD] = grad_q[h * SPAN : (h + 1) * SPAN]
        return done

    lax.fori_loop(0, halves, one_span, 0)

    entry = n_spans
    for out in outs:

        def send(j, carry, out=out, entry=entry):
            out[j] = acc_s[span_at(entry + j), :].astype(jnp.bfloat16)
            return carry

        lax.fori_loop(0, out.shape[0], send, 0)
        entry += out.shape[0]


def on_chip(arrays):
    return [pltpu.with_memory_space_constraint(x, pltpu.VMEM) for x in arrays]


def attend(table, limit, queries, grads, blocks):
    smem = pl.BlockSpec(memory_space=pltpu.SMEM)
    vmem = pl.BlockSpec(memory_space=pltpu.VMEM)
    shard = queries.shape[0]
    n_slots = sum(x.shape[0] for x in blocks) // 4
    tokens = 4 * n_slots * shard
    wide = limit.shape[-1]

    def part(n):
        return pltpu.VMEM((n * n_slots, SPAN, 2 * HEAD), jnp.bfloat16)

    rows_like = jax.ShapeDtypeStruct(queries.shape, jnp.bfloat16)
    return pl.pallas_call(
        functools.partial(attention_kernel, len(blocks)),
        name="attention",
        out_shape=(rows_like, rows_like, part(1), part(1), part(1), part(1), part(2), part(2)),
        in_specs=[smem] + [vmem] * (3 + len(blocks)),
        out_specs=[vmem] * 8,
        compiler_params=pltpu.CompilerParams(vmem_limit_bytes=28 * 2**20),
        scratch_shapes=[
            pltpu.VMEM((tokens, 2 * HEAD), jnp.bfloat16),
            pltpu.VMEM((tokens, 2 * HEAD), jnp.float32),
            pltpu.VMEM((tokens, wide), jnp.float32),
            pltpu.VMEM((wide, HEAD), jnp.bfloat16),
            pltpu.VMEM((wide, HEAD), jnp.bfloat16),
            pltpu.VMEM((HEAD, wide), jnp.float32),
        ],
    )(table, limit, queries, grads, *on_chip(blocks))


def strips_kernel(at_ref, rows_ref, *refs):
    outs, turned = refs[:4], refs[4]
    n_z, part, _ = outs[0].shape
    for i in range(n_z):
        turned[...] = rows_ref[:, i * 4 * part : (i + 1) * 4 * part].astype(jnp.float32).T
        for k, out in enumerate(outs):
            start = pl.multiple_of(at_ref[k] * part, 16)
            out[i] = turned[pl.ds(start, part), :].astype(jnp.bfloat16)


def strips_of(at, rows, n_z):
    shard, width = rows.shape
    part = width // (4 * n_z)
    vmem = pl.BlockSpec(memory_space=pltpu.VMEM)
    return pl.pallas_call(
        strips_kernel,
        name="strips",
        out_shape=(jax.ShapeDtypeStruct((n_z, part, shard), jnp.bfloat16),) * 4,
        in_specs=[pl.BlockSpec(memory_space=pltpu.SMEM), vmem],
        out_specs=[vmem] * 4,
        scratch_shapes=[pltpu.VMEM((4 * part, shard), jnp.float32)],
        compiler_params=pltpu.CompilerParams(vmem_limit_bytes=10 * 2**20),
    )(at, rows)


def grad_w_kernel(z_ref, *refs):
    strips, grads, outs = refs[:4], refs[4:8], refs[8:]
    n_z = strips[0].shape[0]
    for k, out in enumerate(outs):
        i = lax.rem(z_ref[0] + k, n_z)
        total = jnp.dot(strips[0][i], grads[0][...], preferred_element_type=jnp.float32)
        for x, y in zip(strips[1:], grads[1:]):
            total += jnp.dot(x[i], y[...], preferred_element_type=jnp.float32)
        out[...] = total.astype(out.dtype)


def grad_w_parts(z, strips, grads):
    n_z, part, _ = strips[0].shape
    vmem = pl.BlockSpec(memory_space=pltpu.VMEM)
    shape = (part, grads[0].shape[1])
    return pl.pallas_call(
        grad_w_kernel,
        name="grad_w",
        out_shape=(jax.ShapeDtypeStruct(shape, jnp.float32),)
        + (jax.ShapeDtypeStruct(shape, jnp.bfloat16),) * (n_z - 1),
        in_specs=[pl.BlockSpec(memory_space=pltpu.SMEM)] + [vmem] * 8,
        out_specs=[vmem] * n_z,
        compiler_params=pltpu.CompilerParams(vmem_limit_bytes=10 * 2**20),
    )(z, *strips, *grads)


def grad_rows_kernel(grad_ref, w_ref, out_ref):
    step = w_ref.shape[0] // 8
    for i in range(8):
        at = slice(i * step, (i + 1) * step)
        out_ref[:, at] = lax.dot_general(
            grad_ref[...], w_ref[at, :], (((1,), (1,)), ((), ())),
            preferred_element_type=jnp.float32,
        ).astype(out_ref.dtype)


def grad_rows_of(grad_kv, weights):
    vmem = pl.BlockSpec(memory_space=pltpu.VMEM)
    return pl.pallas_call(
        grad_rows_kernel,
        name="grad_rows",
        out_shape=pltpu.VMEM((grad_kv.shape[0], weights.shape[0]), jnp.bfloat16),
        in_specs=[vmem, vmem],
        out_specs=vmem,
        compiler_params=pltpu.CompilerParams(vmem_limit_bytes=8 * 2**20),
    )(*on_chip((grad_kv, weights)))


def total_kernel(terms_ref, out_ref):
    total = terms_ref[0].astype(jnp.float32)
    for i in range(1, terms_ref.shape[0]):
        total += terms_ref[i].astype(jnp.float32)
    out_ref[...] = total.astype(out_ref.dtype)


def total_of(terms):
    vmem = pl.BlockSpec(memory_space=pltpu.VMEM)
    return pl.pallas_call(
        total_kernel,
        name="total",
        out_shape=jax.ShapeDtypeStruct(terms.shape[1:], terms.dtype),
        in_specs=[vmem],
        out_specs=vmem,
        compiler_params=pltpu.CompilerParams(vmem_limit_bytes=4 * 2**20),
    )(*on_chip((terms,)))


def on_device(
    n_z, activations, queries, key_weight, value_weight, output_gradient, span_order, doc_ids
):
    n_ten = 8
    own_rows, width = activations.shape
    shard = own_rows * n_ten
    spans = span_order.shape[0]
    per_shard = shard // SPAN
    heads = queries.shape[1] // HEAD
    z, xl, c = (lax.axis_index(a) for a in CTX)
    swap = [(0, 1), (1, 0)]
    up = [(i, (i + 1) % n_z) for i in range(n_z)]
    down = [(i, (i - 1) % n_z) for i in range(n_z)]

    dz = jnp.array([d for d, _ in brought(n_z)], jnp.int32)
    side = jnp.array([x for _, x in brought(n_z)], jnp.int32)
    halves = jnp.arange(per_shard, dtype=jnp.int32)
    in_near = (((z - dz) % n_z) * 4 + (xl ^ side) * 2)[:, None] * per_shard + halves[None, :]
    steps = jnp.arange(n_z, dtype=jnp.int32)
    sides = (xl ^ jnp.arange(2, dtype=jnp.int32)) * 2
    out_0 = (((z - steps) % n_z) * 4)[None, :] + sides[:, None]
    out_1 = (steps * 4)[:, None] + sides[None, :]
    spans_of = jnp.concatenate(
        [
            (in_near + c * per_shard).reshape(-1),
            (in_near + (1 - c) * per_shard).reshape(-1),
            ((out_0 + c) * per_shard).reshape(-1),
            ((out_0 + 1 - c) * per_shard).reshape(-1),
            ((out_1 + c) * per_shard + 1).reshape(-1),
            ((out_1 + 1 - c) * per_shard + 1).reshape(-1),
        ]
    )
    ids = jnp.arange(spans, dtype=jnp.int32)
    places = jnp.sum(jnp.where(spans_of[:, None] == ids[None, :], span_order[None, :], 0), axis=1)
    first_row = (z * 4 + xl * 2 + c) * shard
    my_order = lax.dynamic_slice_in_dim(span_order, first_row // SPAN, per_shard)
    my_doc = lax.dynamic_slice_in_dim(doc_ids, first_row, shard)
    my_first = jnp.sum((doc_ids[None, :] < my_doc[:, None]).astype(jnp.int32), axis=1)
    my_first = my_first.reshape(per_shard, SPAN)
    my_pos = my_order[:, None] * SPAN + jnp.arange(SPAN, dtype=jnp.int32)[None, :]
    lo, hi = jnp.min(my_first, axis=1) // BLOCK, my_pos[:, -1] // BLOCK + 1
    full_lo = jnp.minimum((jnp.max(my_first, axis=1) + BLOCK - 1) // BLOCK, hi)
    full_hi = jnp.maximum((my_pos[:, 0] + 1) // BLOCK, full_lo)
    bound = jnp.stack([lo, full_lo, full_hi, hi], axis=1)
    table = jnp.concatenate([places, bound.reshape(-1)])
    wide = -(-heads * SPAN // 128) * 128
    pad = wide - heads * SPAN
    limit = jnp.stack(
        [
            jnp.pad(jnp.tile(my_first, (1, heads)), ((0, 0), (0, pad)), constant_values=1),
            jnp.pad(jnp.tile(my_pos, (1, heads)), ((0, 0), (0, pad))),
        ],
        axis=1,
    ).reshape(per_shard, 2, 1, wide)

    def low(x):
        return x.astype(jnp.bfloat16)

    def add(x, y):
        return low(x.astype(jnp.float32) + y.astype(jnp.float32))

    rows = lax.all_to_all(
        jnp.broadcast_to(activations[None], (n_ten, own_rows, width)), TEN, 0, 0
    ).reshape(shard, width)
    weights = jnp.concatenate([key_weight, value_weight], axis=1)
    rows, weights, table, limit = lax.optimization_barrier((rows, weights, table, limit))
    kv = low(jnp.dot(rows, weights, preferred_element_type=jnp.float32))
    beside = lax.ppermute(kv, "xl", swap)
    pair = jnp.stack([kv, beside])
    near = [pair]
    a = b = pair
    for _ in range(1, n_z // 2):
        a = lax.ppermute(a, "z", up)
        b = lax.ppermute(b, "z", down)
        near += [a, b]
    a = lax.ppermute(a[:1], "z", up)
    b = lax.ppermute(b[1:], "z", down)
    near = [jnp.concatenate(near[:5]), jnp.concatenate(near[5:]), jnp.concatenate([a, b])]
    far = []
    for x in near:
        far.append(lax.ppermute(x, "c", swap))

    around = jnp.stack([xl * 2 + c, xl * 2 + 1 - c, (1 - xl) * 2 + c, (1 - xl) * 2 + 1 - c])
    keep, give_c, give_x, give_cx = strips_of(around, rows, n_z)
    got_x = lax.ppermute(give_x, "xl", swap)
    got_c, got_cx = (lax.ppermute(t, "c", swap) for t in (give_c, give_cx))
    got_cx = lax.ppermute(got_cx, "xl", swap)
    strips = (keep, got_c, got_x, got_cx)

    attended, grad_queries, *parts = attend(table, limit, queries, output_gradient, [*near, *far])

    near_00, near_01, far_00, far_01, near_1, far_1 = parts
    far_01 = lax.ppermute(far_01, "c", swap)
    far_1 = lax.ppermute(far_1, "c", swap)
    far_00 = lax.ppermute(far_00, "c", swap)
    part_0 = lax.ppermute(add(near_01, far_01), "xl", swap)
    part_1 = add(near_1, far_1).reshape(n_z, 2, SPAN, 2 * HEAD)
    part_1 = lax.all_to_all(part_1, "z", 0, 0)
    part_0 = near_00.astype(jnp.float32) + far_00.astype(jnp.float32) + part_0.astype(jnp.float32)
    own_0 = part_0[0]
    for k in sorted(range(1, n_z), key=lambda k: -min(k, n_z - k)):
        shift = [(i, (i - k) % n_z) for i in range(n_z)]
        own_0 = own_0 + lax.ppermute(low(part_0[k]), "z", shift).astype(jnp.float32)
    part_1 = jnp.sum(part_1.astype(jnp.float32), axis=0)
    own_1 = part_1[0] + lax.ppermute(low(part_1[1]), "xl", swap).astype(jnp.float32)
    grad_kv = low(jnp.concatenate([own_0, own_1], axis=0))

    beside = lax.ppermute(grad_kv, "xl", swap)
    across = lax.ppermute(grad_kv, "c", swap)
    corner = lax.ppermute(beside, "c", swap)
    grad_rows = grad_rows_of(grad_kv, weights)
    terms = lax.all_to_all(grad_rows.reshape(n_ten, own_rows, width), TEN, 0, 0)

    grad_w, *sent = grad_w_parts(z[None], strips, (grad_kv, across, beside, corner))
    sent = sorted(enumerate(sent, 1), key=lambda kx: -min(kx[0], n_z - kx[0]))
    for k, x in sent:
        shift = [(i, (i + k) % n_z) for i in range(n_z)]
        grad_w = grad_w + lax.ppermute(x, "z", shift).astype(jnp.float32)
    grad_inputs = total_of(terms)
    return attended, grad_queries, grad_inputs, grad_w[:, :HEAD], grad_w[:, HEAD:]


def solution(mesh):
    n_z = mesh.shape["context"] // 4
    fine = Mesh(mesh.devices.reshape(n_z, 2, 2, 2, 4), CTX + TEN)

    def body(*args):
        return on_device(n_z, *args)

    return jax.shard_map(
        body,
        mesh=fine,
        in_specs=(
            P(CTX + TEN, None),
            P(CTX, TEN),
            P(None, TEN),
            P(None, TEN),
            P(CTX, TEN),
            P(),
            P(),
        ),
        out_specs=(
            P(CTX, TEN),
            P(CTX, TEN),
            P(CTX + TEN, None),
            P(CTX, TEN),
            P(CTX, TEN),
        ),
        check_vma=False,
    )
```

profile of v0, /device:TPU:6, one launch (start us, length us, event | category | flops | bytes accessed | tf_op | source)
XLA Modules:
  0.0 228.4 jit_solution(8398793877723149675)
XLA Ops:
  0.6 2.4 %broadcast_in_dim.12 = bf16[8,24,5120]{2,1,0:T(8,128)(2,1)} broadcast(bf16[24,5120]{1,0:T(8,128)(2,1)} %param.9), dimensions={1,2} | broadcast | bytes 2211840 | tf_op jit(solution)/shard_map/broadcast_in_dim | solution.py:333
  3.1 7.6 %all-to-all-start = ((bf16[8,24,5120]{2,1,0:T(8,128)(2,1)}), bf16[8,24,5120]{2,1,0:T(8,128)(2,1)}, u32[]{:S(2)}, u32[]{:S(2)}) async-start(bf16[8,24,5120]{2,1,0:T(8,128)(2,1)} %broadcast_in_dim.12), calls=%async_computation | async-start | bytes 3932160 | tf_op jit(solution)/shard_map/all_to_all | solution.py:332
  10.8 0.6 convert_reduce_fusion
  11.5 0.2 fusion.30
  11.8 0.1 copy.18
  13.1 0.1 select_reduce_fusion
  13.2 2.0 pad_maximum_fusion.w_ref
  15.2 19.6 %all-to-all-done = bf16[8,24,5120]{2,1,0:T(8,128)(2,1)} async-done(((bf16[8,24,5120]{2,1,0:T(8,128)(2,1)}), bf16[8,24,5120]{2,1,0:T(8,128)(2,1)}, u32[]{:S(2)}, u32[]{:S(2)}) %all-to-all-start) | async-done | bytes 1966112 | tf_op jit(solution)/shard_map/all_to_all | solution.py:332
  34.8 2.2 constant_dynamic-update-slice_fusion.5
  37.1 0.9 collective-permute-start
  38.0 3.8 %collective-permute-done = bf16[192,256]{1,0:T(8,128)(2,1)S(1)} collective-permute-done((bf16[192,256]{1,0:T(8,128)(2,1)S(1)}, bf16[192,256]{1,0:T(8,128)(2,1)S(1)}, u32[]{:S(2)}, u32[]{:S(2)}) %collective-permute-start) | collective-permute-done | bytes 98336 | tf_op jit(solution)/shard_map/ppermute | solution.py:338
  41.8 2.0 collective-permute-start.1
  43.8 4.0 %collective-permute-start.2 = (bf16[2,192,256]{2,1,0:T(8,128)(2,1)S(1)}, bf16[2,192,256]{2,1,0:T(8,128)(2,1)S(1)}, u32[]{:S(2)}, u32[]{:S(2)}) collective-permute-start(bf16[2,192,256]{2,1,0:T(8,128)(2,1)S(1)} %pad_maximum_fusion.1), channel_id=1, source_target_pairs={{0,224},{32,0},{64,32},{96,64},{128,96},{160,128},{192,160},{224,1... | collective-permute-start | bytes 589832 | tf_op jit(solution)/shard_map/ppermute | solution.py:344
  47.8 3.6 %collective-permute-done.1 = bf16[2,192,256]{2,1,0:T(8,128)(2,1)S(1)} collective-permute-done((bf16[2,192,256]{2,1,0:T(8,128)(2,1)S(1)}, bf16[2,192,256]{2,1,0:T(8,128)(2,1)S(1)}, u32[]{:S(2)}, u32[]{:S(2)}) %collective-permute-start.1) | collective-permute-done | bytes 196640 | tf_op jit(solution)/shard_map/ppermute | solution.py:343
  51.4 3.3 %collective-permute-start.4 = (bf16[2,192,256]{2,1,0:T(8,128)(2,1)S(1)}, bf16[2,192,256]{2,1,0:T(8,128)(2,1)S(1)}, u32[]{:S(2)}, u32[]{:S(2)}) collective-permute-start(bf16[2,192,256]{2,1,0:T(8,128)(2,1)S(1)} %collective-permute-done.2), channel_id=1, source_target_pairs={{0,224},{32,0},{64,32},{96,64},{128,96},{160,128},{192,160},{224,1... | collective-permute-start | bytes 589832 | tf_op jit(solution)/shard_map/ppermute | solution.py:344
  54.8 3.5 %collective-permute-done.3 = bf16[2,192,256]{2,1,0:T(8,128)(2,1)S(1)} collective-permute-done((bf16[2,192,256]{2,1,0:T(8,128)(2,1)S(1)}, bf16[2,192,256]{2,1,0:T(8,128)(2,1)S(1)}, u32[]{:S(2)}, u32[]{:S(2)}) %collective-permute-start.3) | collective-permute-done | bytes 196640 | tf_op jit(solution)/shard_map/ppermute | solution.py:343
  58.3 0.1 collective-permute-start.9
  58.5 3.4 %collective-permute-start.6 = (bf16[2,192,256]{2,1,0:T(8,128)(2,1)S(1)}, bf16[2,192,256]{2,1,0:T(8,128)(2,1)S(1)}, u32[]{:S(2)}, u32[]{:S(2)}) collective-permute-start(bf16[2,192,256]{2,1,0:T(8,128)(2,1)S(1)} %collective-permute-done.4), channel_id=1, source_target_pairs={{0,224},{32,0},{64,32},{96,64},{128,96},{160,128},{192,160},{224,1... | collective-permute-start | bytes 589832 | tf_op jit(solution)/shard_map/ppermute | solution.py:344
  61.9 5.4 %collective-permute-done.5 = bf16[2,192,256]{2,1,0:T(8,128)(2,1)S(1)} collective-permute-done((bf16[2,192,256]{2,1,0:T(8,128)(2,1)S(1)}, bf16[2,192,256]{2,1,0:T(8,128)(2,1)S(1)}, u32[]{:S(2)}, u32[]{:S(2)}) %collective-permute-start.5) | collective-permute-done | bytes 196640 | tf_op jit(solution)/shard_map/ppermute | solution.py:343
  67.4 3.3 %collective-permute-start.8 = (bf16[1,192,256]{2,1,0:T(8,128)(2,1)S(1)}, bf16[1,192,256]{2,1,0:T(8,128)(2,1)S(1)}, u32[]{:S(2)}, u32[]{:S(2)}) collective-permute-start(bf16[1,192,256]{2,1,0:T(8,128)(2,1)S(1)} %slice.75), channel_id=1, source_target_pairs={{0,224},{32,0},{64,32},{96,64},{128,96},{160,128},{192,160},{224,1... | collective-permute-start | bytes 294920 | tf_op jit(solution)/shard_map/ppermute | solution.py:347
  70.7 0.1 collective-permute-start.10
  70.8 2.4 %collective-permute-done.7 = bf16[1,192,256]{2,1,0:T(8,128)(2,1)S(1)} collective-permute-done((bf16[1,192,256]{2,1,0:T(8,128)(2,1)S(1)}, bf16[1,192,256]{2,1,0:T(8,128)(2,1)S(1)}, u32[]{:S(2)}, u32[]{:S(2)}) %collective-permute-start.7) | collective-permute-done | bytes 98336 | tf_op jit(solution)/shard_map/ppermute | solution.py:346
  73.2 0.3 collective-permute-start.11
  73.5 1.4 collective-permute-done.11.refs_5_
  75.0 13.2 %attention.1 = (bf16[192,640]{1,0:T(8,128)(2,1)}, bf16[192,640]{1,0:T(8,128)(2,1)}, bf16[8,96,256]{2,1,0:T(8,128)(2,1)S(1)}, bf16[8,96,256]{2,1,0:T(8,128)(2,1)S...) custom-call(s32[136]{0:T(256)S(1)} %pad_add_fusion.2.table_ref, ...), custom_call_target="tpu_custom_call" | custom-call | tf_op jit(solution)/shard_map/attention/pallas_call | solution.py:161
  88.1 1.0 collective-permute-start.22
  89.2 1.9 collective-permute-done.22
  91.1 1.1 add_convert_fusion
  92.2 8.9 %all-to-all-start.1 = ((bf16[8,2,96,256]{3,2,1,0:T(8,128)(2,1)}), bf16[8,2,96,256]{3,2,1,0:T(8,128)(2,1)}, u32[]{:S(2)}, u32[]{:S(2)}) async-start(bf16[8,2,96,256]{3,2,1,0:T(8,128)(2,1)} %bitcast.69), calls=%async_computation.1 | async-start | bytes 1572864 | tf_op jit(solution)/shard_map/all_to_all | solution.py:368
  101.1 1.9 add_convert_fusion.1
  102.9 5.6 %collective-permute-start.14 = (bf16[8,96,256]{2,1,0:T(8,128)(2,1)}, bf16[8,96,256]{2,1,0:T(8,128)(2,1)S(1)}, u32[]{:S(2)}, u32[]{:S(2)}) collective-permute-start(bf16[8,96,256]{2,1,0:T(8,128)(2,1)} %add_convert_fusion.1), channel_id=1, source_target_pairs={{0,16},{16,0},{1,17},{17,1},{2,18},{18,2},{3,19},{19,3},{4,20},{20... | collective-permute-start | bytes 1179656 | tf_op jit(solution)/shard_map/ppermute | solution.py:366
  108.5 9.9 %collective-permute-done.14 = bf16[8,96,256]{2,1,0:T(8,128)(2,1)S(1)} collective-permute-done((bf16[8,96,256]{2,1,0:T(8,128)(2,1)}, bf16[8,96,256]{2,1,0:T(8,128)(2,1)S(1)}, u32[]{:S(2)}, u32[]{:S(2)}) %collective-permute-start.14) | collective-permute-done | bytes 393248 | tf_op jit(solution)/shard_map/ppermute | solution.py:366
  118.4 2.0 fusion.31
  120.5 6.0 %collective-permute-start.15 = (bf16[96,256]{1,0:T(8,128)(2,1)S(1)}, bf16[96,256]{1,0:T(8,128)(2,1)S(1)}, u32[]{:S(2)}, u32[]{:S(2)}) collective-permute-start(bf16[96,256]{1,0:T(8,128)(2,1)S(1)} %get-tuple-element.60), channel_id=1, source_target_pairs={{0,128},{32,160},{64,192},{96,224},{128,0},{160,32},{192,64},{224,... | collective-permute-start | bytes 147464 | tf_op jit(solution)/shard_map/ppermute | solution.py:373
  126.5 0.6 collective-permute-start.16
  127.0 3.3 %collective-permute-start.17 = (bf16[96,256]{1,0:T(8,128)(2,1)S(1)}, bf16[96,256]{1,0:T(8,128)(2,1)S(1)}, u32[]{:S(2)}, u32[]{:S(2)}) collective-permute-start(bf16[96,256]{1,0:T(8,128)(2,1)S(1)} %get-tuple-element.65), channel_id=1, source_target_pairs={{0,96},{32,128},{64,160},{96,192},{128,224},{160,0},{192,32},{224,... | collective-permute-start | bytes 147464 | tf_op jit(solution)/shard_map/ppermute | solution.py:373
  130.3 1.8 collective-permute-start.18
  132.1 1.2 collective-permute-start.19
  133.2 1.3 convert_reduce_fusion.1
  134.5 3.1 %collective-permute-start.20 = (bf16[96,256]{1,0:T(8,128)(2,1)S(1)}, bf16[96,256]{1,0:T(8,128)(2,1)S(1)}, u32[]{:S(2)}, u32[]{:S(2)}) collective-permute-start(bf16[96,256]{1,0:T(8,128)(2,1)S(1)} %get-tuple-element.62), channel_id=1, source_target_pairs={{0,224},{32,0},{64,32},{96,64},{128,96},{160,128},{192,160},{224,1... | collective-permute-start | bytes 147464 | tf_op jit(solution)/shard_map/ppermute | solution.py:373
  137.6 1.8 collective-permute-start.23
  139.4 3.4 %collective-permute-done.21 = bf16[96,256]{1,0:T(8,128)(2,1)S(1)} collective-permute-done((bf16[96,256]{1,0:T(8,128)(2,1)S(1)}, bf16[96,256]{1,0:T(8,128)(2,1)S(1)}, u32[]{:S(2)}, u32[]{:S(2)}) %collective-permute-start.21) | collective-permute-done | bytes 49184 | tf_op jit(solution)/shard_map/ppermute | solution.py:373
  142.9 0.9 fusion.9
  143.9 1.0 grad_rows.1
  144.9 1.3 copy-done
  146.2 6.3 %all-to-all-start.2 = ((bf16[8,24,5120]{2,1,0:T(8,128)(2,1)}), bf16[8,24,5120]{2,1,0:T(8,128)(2,1)S(1)}, u32[]{:S(2)}, u32[]{:S(2)}) async-start(bf16[8,24,5120]{2,1,0:T(8,128)(2,1)} %bitcast.68), calls=%async_computation.2 | async-start | bytes 3932160 | tf_op jit(solution)/shard_map/all_to_all | solution.py:382
  152.5 2.5 %strips.1 = (bf16[8,160,192]{2,1,0:T(8,128)(2,1)S(1)}, bf16[8,160,192]{2,1,0:T(8,128)(2,1)S(1)}, bf16[8,160,192]{2,1,0:T(8,128)(2,1)S(1)}, bf16[8,160,192]{2,1,0:T(8,128)(2,1)S(1)}) custom-call(s32[4]{0:T(128)S(1)} %pad_add_fusion.3.at_ref, bf16[192,5120]{1,0:T(8,128)(2,1)} %bitcast.rows_ref), custom_call_target="tpu_custom_call" | custom-call | tf_op jit(solution)/shard_map/strips/pallas_call | solution.py:193
  155.0 0.1 collective-permute-start.26
  155.1 0.5 collective-permute-start.24
  155.6 1.7 collective-permute-start.25
  157.4 1.6 collective-permute-start.27
  159.0 0.4 collective-permute-start.29
  159.4 43.5 %collective-permute-done.29.refs_6_ = bf16[192,256]{1,0:T(8,128)(2,1)S(1)} collective-permute-done((bf16[192,256]{1,0:T(8,128)(2,1)S(1)}, bf16[192,256]{1,0:T(8,128)(2,1)S(1)}, u32[]{:S(2)}, u32[]{:S(2)}) %collective-permute-start.29) | collective-permute-done | bytes 98336 | tf_op jit(solution)/shard_map/ppermute | solution.py:378
  202.9 1.3 collective-permute-done.30.refs_7_
  204.2 0.8 grad_w.1
  205.0 3.3 %collective-permute-start.31 = (bf16[160,256]{1,0:T(8,128)(2,1)S(1)}, bf16[160,256]{1,0:T(8,128)(2,1)S(1)}, u32[]{:S(2)}, u32[]{:S(2)}) collective-permute-start(bf16[160,256]{1,0:T(8,128)(2,1)S(1)} %get-tuple-element.46), channel_id=1, source_target_pairs={{0,128},{32,160},{64,192},{96,224},{128,0},{160,32},{192,64},{224,... | collective-permute-start | bytes 245768 | tf_op jit(solution)/shard_map/ppermute | solution.py:388
  208.3 1.2 collective-permute-start.32
  209.5 3.8 %collective-permute-start.33 = (bf16[160,256]{1,0:T(8,128)(2,1)S(1)}, bf16[160,256]{1,0:T(8,128)(2,1)S(1)}, u32[]{:S(2)}, u32[]{:S(2)}) collective-permute-start(bf16[160,256]{1,0:T(8,128)(2,1)S(1)} %get-tuple-element.48), channel_id=1, source_target_pairs={{0,160},{32,192},{64,224},{96,0},{128,32},{160,64},{192,96},{224,1... | collective-permute-start | bytes 245768 | tf_op jit(solution)/shard_map/ppermute | solution.py:388
  213.4 4.1 %collective-permute-start.35 = (bf16[160,256]{1,0:T(8,128)(2,1)S(1)}, bf16[160,256]{1,0:T(8,128)(2,1)S(1)}, u32[]{:S(2)}, u32[]{:S(2)}) collective-permute-start(bf16[160,256]{1,0:T(8,128)(2,1)S(1)} %get-tuple-element.50), channel_id=1, source_target_pairs={{0,192},{32,224},{64,0},{96,32},{128,64},{160,96},{192,128},{224,1... | collective-permute-start | bytes 245768 | tf_op jit(solution)/shard_map/ppermute | solution.py:388
  217.5 4.7 %collective-permute-done.32 = bf16[160,256]{1,0:T(8,128)(2,1)S(1)} collective-permute-done((bf16[160,256]{1,0:T(8,128)(2,1)S(1)}, bf16[160,256]{1,0:T(8,128)(2,1)S(1)}, u32[]{:S(2)}, u32[]{:S(2)}) %collective-permute-start.32) | collective-permute-done | bytes 81952 | tf_op jit(solution)/shard_map/ppermute | solution.py:388
  222.3 0.9 collective-permute-done.36
  223.1 3.5 %collective-permute-done.37 = bf16[160,256]{1,0:T(8,128)(2,1)S(1)} collective-permute-done((bf16[160,256]{1,0:T(8,128)(2,1)S(1)}, bf16[160,256]{1,0:T(8,128)(2,1)S(1)}, u32[]{:S(2)}, u32[]{:S(2)}) %collective-permute-start.37) | collective-permute-done | bytes 81952 | tf_op jit(solution)/shard_map/ppermute | solution.py:388
  226.7 0.7 fusion.34
  227.4 0.9 total.1
  (103 shorter events, 2.2 us)
Async XLA Ops:
  3.1 7.6 %copy-start.7 = (s32[64]{0:T(128)S(1)}, s32[64]{0:T(128)}, u32[]{:S(2)}) copy-start(s32[64]{0:T(128)} %param.14) | copy-start | bytes 772
  3.1 7.7 %copy-start.4 = (s32[6144]{0:T(1024)S(1)}, s32[6144]{0:T(1024)}, u32[]{:S(2)}) copy-start(s32[6144]{0:T(1024)} %param.15) | copy-start | bytes 73732
  3.1 8.9 %copy-start.5 = (s32[16]{0:T(128)S(1)}, s32[16]{0:T(128)}, u32[]{:S(2)}) copy-start(s32[16]{0:T(128)} %constant.103.clone) | copy-start | bytes 196
  3.1 8.9 %copy-start.6 = (s32[16]{0:T(128)S(1)}, s32[16]{0:T(128)}, u32[]{:S(2)}) copy-start(s32[16]{0:T(128)} %constant.109) | copy-start | bytes 196
  3.1 31.8 %all-to-all-start = ((bf16[8,24,5120]{2,1,0:T(8,128)(2,1)}), bf16[8,24,5120]{2,1,0:T(8,128)(2,1)}, u32[]{:S(2)}, u32[]{:S(2)}) async-start(bf16[8,24,5120]{2,1,0:T(8,128)(2,1)} %broadcast_in_dim.12), calls=%async_computation | async-start | bytes 3932160 | tf_op jit(solution)/shard_map/all_to_all | solution.py:332
  37.1 37.9 %copy-start.1 = (bf16[192,640]{1,0:T(8,128)(2,1)S(1)}, bf16[192,640]{1,0:T(8,128)(2,1)}, u32[]{:S(2)}) copy-start(bf16[192,640]{1,0:T(8,128)(2,1)} %q_ref.1) | copy-start | bytes 737284
  37.1 37.9 %copy-start.2 = (bf16[192,640]{1,0:T(8,128)(2,1)S(1)}, bf16[192,640]{1,0:T(8,128)(2,1)}, u32[]{:S(2)}) copy-start(bf16[192,640]{1,0:T(8,128)(2,1)} %g_ref.1) | copy-start | bytes 737284
  37.1 4.7 %collective-permute-start = (bf16[192,256]{1,0:T(8,128)(2,1)S(1)}, bf16[192,256]{1,0:T(8,128)(2,1)S(1)}, u32[]{:S(2)}, u32[]{:S(2)}) collective-permute-start(bf16[192,256]{1,0:T(8,128)(2,1)S(1)} %get-tuple-element.76), channel_id=1, source_target_pairs={{0,16},{16,0},{1,17},{17,1},{2,18},{18,2},{3,19},{19,3},{4,20},{20... | collective-permute-start | bytes 294920 | tf_op jit(solution)/shard_map/ppermute | solution.py:338
  41.8 9.6 %collective-permute-start.1 = (bf16[2,192,256]{2,1,0:T(8,128)(2,1)S(1)}, bf16[2,192,256]{2,1,0:T(8,128)(2,1)S(1)}, u32[]{:S(2)}, u32[]{:S(2)}) collective-permute-start(bf16[2,192,256]{2,1,0:T(8,128)(2,1)S(1)} %pad_maximum_fusion.1), channel_id=1, source_target_pairs={{0,32},{32,64},{64,96},{96,128},{128,160},{160,192},{192,224},{224... | collective-permute-start | bytes 589832 | tf_op jit(solution)/shard_map/ppermute | solution.py:343
  43.8 7.6 %collective-permute-start.2 = (bf16[2,192,256]{2,1,0:T(8,128)(2,1)S(1)}, bf16[2,192,256]{2,1,0:T(8,128)(2,1)S(1)}, u32[]{:S(2)}, u32[]{:S(2)}) collective-permute-start(bf16[2,192,256]{2,1,0:T(8,128)(2,1)S(1)} %pad_maximum_fusion.1), channel_id=1, source_target_pairs={{0,224},{32,0},{64,32},{96,64},{128,96},{160,128},{192,160},{224,1... | collective-permute-start | bytes 589832 | tf_op jit(solution)/shard_map/ppermute | solution.py:344
  51.4 6.9 %collective-permute-start.3 = (bf16[2,192,256]{2,1,0:T(8,128)(2,1)S(1)}, bf16[2,192,256]{2,1,0:T(8,128)(2,1)S(1)}, u32[]{:S(2)}, u32[]{:S(2)}) collective-permute-start(bf16[2,192,256]{2,1,0:T(8,128)(2,1)S(1)} %collective-permute-done.1), channel_id=1, source_target_pairs={{0,32},{32,64},{64,96},{96,128},{128,160},{160,192},{192,224},{224... | collective-permute-start | bytes 589832 | tf_op jit(solution)/shard_map/ppermute | solution.py:343
  51.4 6.9 %collective-permute-start.4 = (bf16[2,192,256]{2,1,0:T(8,128)(2,1)S(1)}, bf16[2,192,256]{2,1,0:T(8,128)(2,1)S(1)}, u32[]{:S(2)}, u32[]{:S(2)}) collective-permute-start(bf16[2,192,256]{2,1,0:T(8,128)(2,1)S(1)} %collective-permute-done.2), channel_id=1, source_target_pairs={{0,224},{32,0},{64,32},{96,64},{128,96},{160,128},{192,160},{224,1... | collective-permute-start | bytes 589832 | tf_op jit(solution)/shard_map/ppermute | solution.py:344
  58.3 16.6 %collective-permute-start.9 = (bf16[10,192,256]{2,1,0:T(8,128)(2,1)S(1)}, bf16[10,192,256]{2,1,0:T(8,128)(2,1)S(1)}, u32[]{:S(2)}, u32[]{:S(2)}) collective-permute-start(bf16[10,192,256]{2,1,0:T(8,128)(2,1)S(1)} %constant_dynamic-update-slice_fusion.refs_0_), channel_id=1, source_target_pairs={{0,8},{8,0},{1,9},{9,1},{2,10},{10,2},{3,11},{11,3},{4,12},{12,4},... | collective-permute-start | bytes 2949128 | tf_op jit(solution)/shard_map/ppermute | solution.py:351
  58.4 8.8 %collective-permute-start.5 = (bf16[2,192,256]{2,1,0:T(8,128)(2,1)S(1)}, bf16[2,192,256]{2,1,0:T(8,128)(2,1)S(1)}, u32[]{:S(2)}, u32[]{:S(2)}) collective-permute-start(bf16[2,192,256]{2,1,0:T(8,128)(2,1)S(1)} %collective-permute-done.3), channel_id=1, source_target_pairs={{0,32},{32,64},{64,96},{96,128},{128,160},{160,192},{192,224},{224... | collective-permute-start | bytes 589832 | tf_op jit(solution)/shard_map/ppermute | solution.py:343
  58.5 8.9 %collective-permute-start.6 = (bf16[2,192,256]{2,1,0:T(8,128)(2,1)S(1)}, bf16[2,192,256]{2,1,0:T(8,128)(2,1)S(1)}, u32[]{:S(2)}, u32[]{:S(2)}) collective-permute-start(bf16[2,192,256]{2,1,0:T(8,128)(2,1)S(1)} %collective-permute-done.4), channel_id=1, source_target_pairs={{0,224},{32,0},{64,32},{96,64},{128,96},{160,128},{192,160},{224,1... | collective-permute-start | bytes 589832 | tf_op jit(solution)/shard_map/ppermute | solution.py:344
  67.3 5.9 %collective-permute-start.7 = (bf16[1,192,256]{2,1,0:T(8,128)(2,1)S(1)}, bf16[1,192,256]{2,1,0:T(8,128)(2,1)S(1)}, u32[]{:S(2)}, u32[]{:S(2)}) collective-permute-start(bf16[1,192,256]{2,1,0:T(8,128)(2,1)S(1)} %slice.74), channel_id=1, source_target_pairs={{0,32},{32,64},{64,96},{96,128},{128,160},{160,192},{192,224},{224... | collective-permute-start | bytes 294920 | tf_op jit(solution)/shard_map/ppermute | solution.py:346
  67.4 5.8 %collective-permute-start.8 = (bf16[1,192,256]{2,1,0:T(8,128)(2,1)S(1)}, bf16[1,192,256]{2,1,0:T(8,128)(2,1)S(1)}, u32[]{:S(2)}, u32[]{:S(2)}) collective-permute-start(bf16[1,192,256]{2,1,0:T(8,128)(2,1)S(1)} %slice.75), channel_id=1, source_target_pairs={{0,224},{32,0},{64,32},{96,64},{128,96},{160,128},{192,160},{224,1... | collective-permute-start | bytes 294920 | tf_op jit(solution)/shard_map/ppermute | solution.py:347
  70.7 4.2 %collective-permute-start.10 = (bf16[4,192,256]{2,1,0:T(8,128)(2,1)S(1)}, bf16[4,192,256]{2,1,0:T(8,128)(2,1)S(1)}, u32[]{:S(2)}, u32[]{:S(2)}) collective-permute-start(bf16[4,192,256]{2,1,0:T(8,128)(2,1)S(1)} %constant_dynamic-update-slice_fusion.6.refs_1_), channel_id=1, source_target_pairs={{0,8},{8,0},{1,9},{9,1},{2,10},{10,2},{3,11},{11,3},{4,12},{12,4},... | collective-permute-start | bytes 1179656 | tf_op jit(solution)/shard_map/ppermute | solution.py:351
  73.2 1.7 collective-permute-start.11
  88.1 4.1 %copy-start.3 = (bf16[8,96,256]{2,1,0:T(8,128)(2,1)}, bf16[8,96,256]{2,1,0:T(8,128)(2,1)S(1)}, u32[]{:S(2)}) copy-start(bf16[8,96,256]{2,1,0:T(8,128)(2,1)S(1)} %get-tuple-element.36) | copy-start | bytes 1179652
  88.1 3.0 %collective-permute-start.22 = (bf16[16,96,256]{2,1,0:T(8,128)(2,1)S(1)}, bf16[16,96,256]{2,1,0:T(8,128)(2,1)S(1)}, u32[]{:S(2)}, u32[]{:S(2)}) collective-permute-start(bf16[16,96,256]{2,1,0:T(8,128)(2,1)S(1)} %get-tuple-element.40), channel_id=1, source_target_pairs={{0,8},{8,0},{1,9},{9,1},{2,10},{10,2},{3,11},{11,3},{4,12},{12,4},... | collective-permute-start | bytes 2359304 | tf_op jit(solution)/shard_map/ppermute | solution.py:364
  89.2 11.9 %collective-permute-start.13 = (bf16[8,96,256]{2,1,0:T(8,128)(2,1)}, bf16[8,96,256]{2,1,0:T(8,128)(2,1)}, u32[]{:S(2)}, u32[]{:S(2)}) collective-permute-start(bf16[8,96,256]{2,1,0:T(8,128)(2,1)} %get-tuple-element.38), channel_id=1, source_target_pairs={{0,8},{8,0},{1,9},{9,1},{2,10},{10,2},{3,11},{11,3},{4,12},{12,4},... | collective-permute-start | bytes 1179656 | tf_op jit(solution)/shard_map/ppermute | solution.py:363
  92.2 41.0 %all-to-all-start.1 = ((bf16[8,2,96,256]{3,2,1,0:T(8,128)(2,1)}), bf16[8,2,96,256]{3,2,1,0:T(8,128)(2,1)}, u32[]{:S(2)}, u32[]{:S(2)}) async-start(bf16[8,2,96,256]{3,2,1,0:T(8,128)(2,1)} %bitcast.69), calls=%async_computation.1 | async-start | bytes 1572864 | tf_op jit(solution)/shard_map/all_to_all | solution.py:368
  101.1 7.4 %collective-permute-start.12 = (bf16[8,96,256]{2,1,0:T(8,128)(2,1)}, bf16[8,96,256]{2,1,0:T(8,128)(2,1)}, u32[]{:S(2)}, u32[]{:S(2)}) collective-permute-start(bf16[8,96,256]{2,1,0:T(8,128)(2,1)} %copy-done.3), channel_id=1, source_target_pairs={{0,8},{8,0},{1,9},{9,1},{2,10},{10,2},{3,11},{11,3},{4,12},{12,4},... | collective-permute-start | bytes 1179656 | tf_op jit(solution)/shard_map/ppermute | solution.py:365
  102.9 15.5 %collective-permute-start.14 = (bf16[8,96,256]{2,1,0:T(8,128)(2,1)}, bf16[8,96,256]{2,1,0:T(8,128)(2,1)S(1)}, u32[]{:S(2)}, u32[]{:S(2)}) collective-permute-start(bf16[8,96,256]{2,1,0:T(8,128)(2,1)} %add_convert_fusion.1), channel_id=1, source_target_pairs={{0,16},{16,0},{1,17},{17,1},{2,18},{18,2},{3,19},{19,3},{4,20},{20... | collective-permute-start | bytes 1179656 | tf_op jit(solution)/shard_map/ppermute | solution.py:366
  120.5 14.0 %collective-permute-start.15 = (bf16[96,256]{1,0:T(8,128)(2,1)S(1)}, bf16[96,256]{1,0:T(8,128)(2,1)S(1)}, u32[]{:S(2)}, u32[]{:S(2)}) collective-permute-start(bf16[96,256]{1,0:T(8,128)(2,1)S(1)} %get-tuple-element.60), channel_id=1, source_target_pairs={{0,128},{32,160},{64,192},{96,224},{128,0},{160,32},{192,64},{224,... | collective-permute-start | bytes 147464 | tf_op jit(solution)/shard_map/ppermute | solution.py:373
  126.5 11.1 %collective-permute-start.16 = (bf16[96,256]{1,0:T(8,128)(2,1)S(1)}, bf16[96,256]{1,0:T(8,128)(2,1)S(1)}, u32[]{:S(2)}, u32[]{:S(2)}) collective-permute-start(bf16[96,256]{1,0:T(8,128)(2,1)S(1)} %get-tuple-element.66), channel_id=1, source_target_pairs={{0,160},{32,192},{64,224},{96,0},{128,32},{160,64},{192,96},{224,1... | collective-permute-start | bytes 147464 | tf_op jit(solution)/shard_map/ppermute | solution.py:373
  127.0 10.5 %collective-permute-start.17 = (bf16[96,256]{1,0:T(8,128)(2,1)S(1)}, bf16[96,256]{1,0:T(8,128)(2,1)S(1)}, u32[]{:S(2)}, u32[]{:S(2)}) collective-permute-start(bf16[96,256]{1,0:T(8,128)(2,1)S(1)} %get-tuple-element.65), channel_id=1, source_target_pairs={{0,96},{32,128},{64,160},{96,192},{128,224},{160,0},{192,32},{224,... | collective-permute-start | bytes 147464 | tf_op jit(solution)/shard_map/ppermute | solution.py:373
  130.3 9.1 %collective-permute-start.18 = (bf16[96,256]{1,0:T(8,128)(2,1)S(1)}, bf16[96,256]{1,0:T(8,128)(2,1)S(1)}, u32[]{:S(2)}, u32[]{:S(2)}) collective-permute-start(bf16[96,256]{1,0:T(8,128)(2,1)S(1)} %get-tuple-element.64), channel_id=1, source_target_pairs={{0,192},{32,224},{64,0},{96,32},{128,64},{160,96},{192,128},{224,1... | collective-permute-start | bytes 147464 | tf_op jit(solution)/shard_map/ppermute | solution.py:373
  132.1 7.3 %collective-permute-start.19 = (bf16[96,256]{1,0:T(8,128)(2,1)S(1)}, bf16[96,256]{1,0:T(8,128)(2,1)S(1)}, u32[]{:S(2)}, u32[]{:S(2)}) collective-permute-start(bf16[96,256]{1,0:T(8,128)(2,1)S(1)} %get-tuple-element.63), channel_id=1, source_target_pairs={{0,64},{32,96},{64,128},{96,160},{128,192},{160,224},{192,0},{224,... | collective-permute-start | bytes 147464 | tf_op jit(solution)/shard_map/ppermute | solution.py:373
  134.5 4.9 %collective-permute-start.20 = (bf16[96,256]{1,0:T(8,128)(2,1)S(1)}, bf16[96,256]{1,0:T(8,128)(2,1)S(1)}, u32[]{:S(2)}, u32[]{:S(2)}) collective-permute-start(bf16[96,256]{1,0:T(8,128)(2,1)S(1)} %get-tuple-element.62), channel_id=1, source_target_pairs={{0,224},{32,0},{64,32},{96,64},{128,96},{160,128},{192,160},{224,1... | collective-permute-start | bytes 147464 | tf_op jit(solution)/shard_map/ppermute | solution.py:373
  137.6 5.3 %collective-permute-start.21 = (bf16[96,256]{1,0:T(8,128)(2,1)S(1)}, bf16[96,256]{1,0:T(8,128)(2,1)S(1)}, u32[]{:S(2)}, u32[]{:S(2)}) collective-permute-start(bf16[96,256]{1,0:T(8,128)(2,1)S(1)} %get-tuple-element.61), channel_id=1, source_target_pairs={{0,32},{32,64},{64,96},{96,128},{128,160},{160,192},{192,224},{224... | collective-permute-start | bytes 147464 | tf_op jit(solution)/shard_map/ppermute | solution.py:373
  137.6 6.2 %collective-permute-start.23 = (bf16[96,256]{1,0:T(8,128)(2,1)S(1)}, bf16[96,256]{1,0:T(8,128)(2,1)S(1)}, u32[]{:S(2)}, u32[]{:S(2)}) collective-permute-start(bf16[96,256]{1,0:T(8,128)(2,1)S(1)} %fusion.10), channel_id=1, source_target_pairs={{0,16},{16,0},{1,17},{17,1},{2,18},{18,2},{3,19},{19,3},{4,20},{20... | collective-permute-start | bytes 147464 | tf_op jit(solution)/shard_map/ppermute | solution.py:375
  144.9 1.3 copy-start
  146.2 81.3 %all-to-all-start.2 = ((bf16[8,24,5120]{2,1,0:T(8,128)(2,1)}), bf16[8,24,5120]{2,1,0:T(8,128)(2,1)S(1)}, u32[]{:S(2)}, u32[]{:S(2)}) async-start(bf16[8,24,5120]{2,1,0:T(8,128)(2,1)} %bitcast.68), calls=%async_computation.2 | async-start | bytes 3932160 | tf_op jit(solution)/shard_map/all_to_all | solution.py:382
  155.0 2.3 %collective-permute-start.26 = (bf16[8,160,192]{2,1,0:T(8,128)(2,1)S(1)}, bf16[8,160,192]{2,1,0:T(8,128)(2,1)S(1)}, u32[]{:S(2)}, u32[]{:S(2)}) collective-permute-start(bf16[8,160,192]{2,1,0:T(8,128)(2,1)S(1)} %get-tuple-element.44), channel_id=1, source_target_pairs={{0,8},{8,0},{1,9},{9,1},{2,10},{10,2},{3,11},{11,3},{4,12},{12,4},... | collective-permute-start | bytes 1474568 | tf_op jit(solution)/shard_map/ppermute | solution.py:356
  155.1 47.7 %collective-permute-start.24 = (bf16[8,160,192]{2,1,0:T(8,128)(2,1)S(1)}, bf16[8,160,192]{2,1,0:T(8,128)(2,1)S(1)}, u32[]{:S(2)}, u32[]{:S(2)}) collective-permute-start(bf16[8,160,192]{2,1,0:T(8,128)(2,1)S(1)} %get-tuple-element.42), channel_id=1, source_target_pairs={{0,8},{8,0},{1,9},{9,1},{2,10},{10,2},{3,11},{11,3},{4,12},{12,4},... | collective-permute-start | bytes 1474568 | tf_op jit(solution)/shard_map/ppermute | solution.py:356
  155.6 47.2 %collective-permute-start.25 = (bf16[8,160,192]{2,1,0:T(8,128)(2,1)S(1)}, bf16[8,160,192]{2,1,0:T(8,128)(2,1)S(1)}, u32[]{:S(2)}, u32[]{:S(2)}) collective-permute-start(bf16[8,160,192]{2,1,0:T(8,128)(2,1)S(1)} %get-tuple-element.43), channel_id=1, source_target_pairs={{0,16},{16,0},{1,17},{17,1},{2,18},{18,2},{3,19},{19,3},{4,20},{20... | collective-permute-start | bytes 1474568 | tf_op jit(solution)/shard_map/ppermute | solution.py:355
  157.4 45.5 %collective-permute-start.27 = (bf16[8,160,192]{2,1,0:T(8,128)(2,1)S(1)}, bf16[8,160,192]{2,1,0:T(8,128)(2,1)S(1)}, u32[]{:S(2)}, u32[]{:S(2)}) collective-permute-start(bf16[8,160,192]{2,1,0:T(8,128)(2,1)S(1)} %collective-permute-done.26), channel_id=1, source_target_pairs={{0,16},{16,0},{1,17},{17,1},{2,18},{18,2},{3,19},{19,3},{4,20},{20... | collective-permute-start | bytes 1474568 | tf_op jit(solution)/shard_map/ppermute | solution.py:357
  159.0 43.9 %collective-permute-start.29 = (bf16[192,256]{1,0:T(8,128)(2,1)S(1)}, bf16[192,256]{1,0:T(8,128)(2,1)S(1)}, u32[]{:S(2)}, u32[]{:S(2)}) collective-permute-start(bf16[192,256]{1,0:T(8,128)(2,1)S(1)} %pad_maximum_fusion.2.grad_ref.refs_4_), channel_id=1, source_target_pairs={{0,16},{16,0},{1,17},{17,1},{2,18},{18,2},{3,19},{19,3},{4,20},{20... | collective-permute-start | bytes 294920 | tf_op jit(solution)/shard_map/ppermute | solution.py:378
  159.4 43.5 %collective-permute-start.28 = (bf16[192,256]{1,0:T(8,128)(2,1)S(1)}, bf16[192,256]{1,0:T(8,128)(2,1)S(1)}, u32[]{:S(2)}, u32[]{:S(2)}) collective-permute-start(bf16[192,256]{1,0:T(8,128)(2,1)S(1)} %pad_maximum_fusion.2.grad_ref.refs_4_), channel_id=1, source_target_pairs={{0,8},{8,0},{1,9},{9,1},{2,10},{10,2},{3,11},{11,3},{4,12},{12,4},... | collective-permute-start | bytes 294920 | tf_op jit(solution)/shard_map/ppermute | solution.py:379
  202.9 1.3 collective-permute-start.30
  205.0 12.5 %collective-permute-start.31 = (bf16[160,256]{1,0:T(8,128)(2,1)S(1)}, bf16[160,256]{1,0:T(8,128)(2,1)S(1)}, u32[]{:S(2)}, u32[]{:S(2)}) collective-permute-start(bf16[160,256]{1,0:T(8,128)(2,1)S(1)} %get-tuple-element.46), channel_id=1, source_target_pairs={{0,128},{32,160},{64,192},{96,224},{128,0},{160,32},{192,64},{224,... | collective-permute-start | bytes 245768 | tf_op jit(solution)/shard_map/ppermute | solution.py:388
  208.3 13.9 %collective-permute-start.32 = (bf16[160,256]{1,0:T(8,128)(2,1)S(1)}, bf16[160,256]{1,0:T(8,128)(2,1)S(1)}, u32[]{:S(2)}, u32[]{:S(2)}) collective-permute-start(bf16[160,256]{1,0:T(8,128)(2,1)S(1)} %get-tuple-element.47), channel_id=1, source_target_pairs={{0,96},{32,128},{64,160},{96,192},{128,224},{160,0},{192,32},{224,... | collective-permute-start | bytes 245768 | tf_op jit(solution)/shard_map/ppermute | solution.py:388
  209.5 12.7 %collective-permute-start.33 = (bf16[160,256]{1,0:T(8,128)(2,1)S(1)}, bf16[160,256]{1,0:T(8,128)(2,1)S(1)}, u32[]{:S(2)}, u32[]{:S(2)}) collective-permute-start(bf16[160,256]{1,0:T(8,128)(2,1)S(1)} %get-tuple-element.48), channel_id=1, source_target_pairs={{0,160},{32,192},{64,224},{96,0},{128,32},{160,64},{192,96},{224,1... | collective-permute-start | bytes 245768 | tf_op jit(solution)/shard_map/ppermute | solution.py:388
  213.4 8.9 %collective-permute-start.34 = (bf16[160,256]{1,0:T(8,128)(2,1)S(1)}, bf16[160,256]{1,0:T(8,128)(2,1)S(1)}, u32[]{:S(2)}, u32[]{:S(2)}) collective-permute-start(bf16[160,256]{1,0:T(8,128)(2,1)S(1)} %get-tuple-element.49), channel_id=1, source_target_pairs={{0,64},{32,96},{64,128},{96,160},{128,192},{160,224},{192,0},{224,... | collective-permute-start | bytes 245768 | tf_op jit(solution)/shard_map/ppermute | solution.py:388
  213.4 8.9 %collective-permute-start.35 = (bf16[160,256]{1,0:T(8,128)(2,1)S(1)}, bf16[160,256]{1,0:T(8,128)(2,1)S(1)}, u32[]{:S(2)}, u32[]{:S(2)}) collective-permute-start(bf16[160,256]{1,0:T(8,128)(2,1)S(1)} %get-tuple-element.50), channel_id=1, source_target_pairs={{0,192},{32,224},{64,0},{96,32},{128,64},{160,96},{192,128},{224,1... | collective-permute-start | bytes 245768 | tf_op jit(solution)/shard_map/ppermute | solution.py:388
  217.5 5.7 %collective-permute-start.36 = (bf16[160,256]{1,0:T(8,128)(2,1)S(1)}, bf16[160,256]{1,0:T(8,128)(2,1)S(1)}, u32[]{:S(2)}, u32[]{:S(2)}) collective-permute-start(bf16[160,256]{1,0:T(8,128)(2,1)S(1)} %get-tuple-element.51), channel_id=1, source_target_pairs={{0,32},{32,64},{64,96},{96,128},{128,160},{160,192},{192,224},{224... | collective-permute-start | bytes 245768 | tf_op jit(solution)/shard_map/ppermute | solution.py:388
  222.2 4.4 %collective-permute-start.37 = (bf16[160,256]{1,0:T(8,128)(2,1)S(1)}, bf16[160,256]{1,0:T(8,128)(2,1)S(1)}, u32[]{:S(2)}, u32[]{:S(2)}) collective-permute-start(bf16[160,256]{1,0:T(8,128)(2,1)S(1)} %get-tuple-element.52), channel_id=1, source_target_pairs={{0,224},{32,0},{64,32},{96,64},{128,96},{160,128},{192,160},{224,1... | collective-permute-start | bytes 245768 | tf_op jit(solution)/shard_map/ppermute | solution.py:388
where the time goes:
time: 229 us; the launch traced here: 228 us
  waiting for transfers between devices  109 us (48%)
  starting transfers between devices  81.3 us (36%)
  Pallas kernels  18.5 us (8%)
  other arithmetic  10.7 us (5%)
  local copies, waits for them, and re-layouts  5.76 us (3%)
    ppermute x1, waiting for transfers between devices, on_device(): beside = lax.ppermute(grad_kv, 'xl', swap)  43.5 us
    all_to_all x1, waiting for transfers between devices, on_device(): lax.all_to_all(jnp.broadcast_to(activations[None], (n_ten, own_rows, widt...  19.6 us
    ppermute x7, starting transfers between devices, on_device(): own_0 = own_0 + lax.ppermute(low(part_0[k]), 'z', shift).astype(jnp.float32)  15.8 us
    pallas_call x1, Pallas kernels, attend(): pl.pallas_call(functools.partial(attention_kernel, len(blocks)), name='at...  13.2 us
    ppermute x7, starting transfers between devices, on_device(): grad_w = grad_w + lax.ppermute(x, 'z', shift).astype(jnp.float32)  12.5 us
    ppermute x3, waiting for transfers between devices, on_device(): a = lax.ppermute(a, 'z', up)  12.5 us
    ppermute x3, starting transfers between devices, on_device(): b = lax.ppermute(b, 'z', down)  10.7 us
    ppermute x1, waiting for transfers between devices, on_device(): part_0 = lax.ppermute(add(near_01, far_01), 'xl', swap)  9.9 us
  transfers between devices with their start and end apart: 41, of which 16 were waited for; matrix products, arithmetic and copies ran while one was open for 6% of the time, Pallas kernels for 1%

commit v1 on v0

--- a/solution.py
+++ b/solution.py
@@ -161,7 +161,7 @@
     return pl.pallas_call(
         functools.partial(attention_kernel, len(blocks)),
         name="attention",
-        out_shape=(rows_like, rows_like, part(1), part(1), part(1), part(1), part(2), part(2)),
+        out_shape=(rows_like, rows_like) + (part(2), part(1), part(1)) * 2,
         in_specs=[smem] + [vmem] * (3 + len(blocks)),
         out_specs=[vmem] * 8,
         compiler_params=pltpu.CompilerParams(vmem_limit_bytes=28 * 2**20),
@@ -287,17 +287,20 @@
     halves = jnp.arange(per_shard, dtype=jnp.int32)
     in_near = (((z - dz) % n_z) * 4 + (xl ^ side) * 2)[:, None] * per_shard + halves[None, :]
     steps = jnp.arange(n_z, dtype=jnp.int32)
-    sides = (xl ^ jnp.arange(2, dtype=jnp.int32)) * 2
-    out_0 = (((z - steps) % n_z) * 4)[None, :] + sides[:, None]
-    out_1 = (steps * 4)[:, None] + sides[None, :]
+    below = ((z - steps) % n_z) * 4
+
+    def sent_at(core):
+        own_side = ((below + xl * 2 + core)[:, None] * per_shard + halves[None, :]).reshape(-1)
+        first = (below + (1 - xl) * 2 + core) * per_shard
+        second = (steps * 4 + (1 - xl) * 2 + core) * per_shard + 1
+        return [own_side, first, second]
+
     spans_of = jnp.concatenate(
         [
             (in_near + c * per_shard).reshape(-1),
             (in_near + (1 - c) * per_shard).reshape(-1),
-            ((out_0 + c) * per_shard).reshape(-1),
-            ((out_0 + 1 - c) * per_shard).reshape(-1),
-            ((out_1 + c) * per_shard + 1).reshape(-1),
-            ((out_1 + 1 - c) * per_shard + 1).reshape(-1),
+            *sent_at(c),
+            *sent_at(1 - c),
         ]
     )
     ids = jnp.arange(spans, dtype=jnp.int32)
@@ -359,21 +362,23 @@
 
     attended, grad_queries, *parts = attend(table, limit, queries, output_gradient, [*near, *far])
 
-    near_00, near_01, far_00, far_01, near_1, far_1 = parts
-    far_01 = lax.ppermute(far_01, "c", swap)
+    near_own, near_0, near_1, far_own, far_0, far_1 = parts
+    far_0 = lax.ppermute(far_0, "c", swap)
     far_1 = lax.ppermute(far_1, "c", swap)
-    far_00 = lax.ppermute(far_00, "c", swap)
-    part_0 = lax.ppermute(add(near_01, far_01), "xl", swap)
-    part_1 = add(near_1, far_1).reshape(n_z, 2, SPAN, 2 * HEAD)
-    part_1 = lax.all_to_all(part_1, "z", 0, 0)
-    part_0 = near_00.astype(jnp.float32) + far_00.astype(jnp.float32) + part_0.astype(jnp.float32)
-    own_0 = part_0[0]
+    far_own = lax.ppermute(far_own, "c", swap)
+    part_0 = lax.ppermute(add(near_0, far_0), "xl", swap)
+    part_1 = lax.all_to_all(add(near_1, far_1), "z", 0, 0)
+    part = near_own.astype(jnp.float32) + far_own.astype(jnp.float32)
+    part = part.reshape(n_z, per_shard, SPAN, 2 * HEAD)
+    part += jnp.pad(part_0[:, None].astype(jnp.float32), ((0, 0), (0, 1), (0, 0), (0, 0)))
+    own = part[0]
     for k in sorted(range(1, n_z), key=lambda k: -min(k, n_z - k)):
         shift = [(i, (i - k) % n_z) for i in range(n_z)]
-        own_0 = own_0 + lax.ppermute(low(part_0[k]), "z", shift).astype(jnp.float32)
-    part_1 = jnp.sum(part_1.astype(jnp.float32), axis=0)
-    own_1 = part_1[0] + lax.ppermute(low(part_1[1]), "xl", swap).astype(jnp.float32)
-    grad_kv = low(jnp.concatenate([own_0, own_1], axis=0))
+        own = own + lax.ppermute(low(part[k]), "z", shift).astype(jnp.float32)
+    part_1 = low(jnp.sum(part_1.astype(jnp.float32), axis=0))
+    part_1 = lax.ppermute(part_1, "xl", swap)
+    own = own + jnp.pad(part_1[None].astype(jnp.float32), ((1, 0), (0, 0), (0, 0)))
+    grad_kv = low(own).reshape(shard, 2 * HEAD)
 
     beside = lax.ppermute(grad_kv, "xl", swap)
     across = lax.ppermute(grad_kv, "c", swap)

time: 229 us -> 227 us (level)
  the two profiles are of different devices: /device:TPU:6 before, /device:TPU:32 now
where the time goes in v1:
time: 227 us; the launch traced here: 224 us
  waiting for transfers between devices  105 us (46%)
  starting transfers between devices  82 us (36%)
  Pallas kernels  16.1 us (7%)
  other arithmetic  11.8 us (5%)
  local copies, waits for them, and re-layouts  6.26 us (3%)
    ppermute x1, waiting for transfers between devices, on_device(): beside = lax.ppermute(grad_kv, 'xl', swap)  45 us
    all_to_all x1, waiting for transfers between devices, on_device(): lax.all_to_all(jnp.broadcast_to(activations[None], (n_ten, own_rows, widt...  20.7 us
    ppermute x7, starting transfers between devices, on_device(): own = own + lax.ppermute(low(part[k]), 'z', shift).astype(jnp.float32)  16.3 us
    ppermute x7, starting transfers between devices, on_device(): grad_w = grad_w + lax.ppermute(x, 'z', shift).astype(jnp.float32)  15.9 us
    ppermute x3, waiting for transfers between devices, on_device(): a = lax.ppermute(a, 'z', up)  12 us
    all_to_all x1, starting transfers between devices, on_device(): part_1 = lax.all_to_all(add(near_1, far_1), 'z', 0, 0)  11.8 us
    pallas_call x1, Pallas kernels, attend(): pl.pallas_call(functools.partial(attention_kernel, len(blocks)), name='at...  10.8 us
    ppermute x3, starting transfers between devices, on_device(): a = lax.ppermute(a, 'z', up)  7.59 us
  transfers between devices with their start and end apart: 41, of which 22 were waited for; matrix products, arithmetic and copies ran while one was open for 6% of the time, Pallas kernels for 1%

profile of v1, /device:TPU:32, one launch (start us, length us, event | category | flops | bytes accessed | tf_op | source)
XLA Modules:
  0.0 224.0 jit_solution(15180732774717449992)
XLA Ops:
  0.6 2.4 %broadcast_in_dim.12 = bf16[8,24,5120]{2,1,0:T(8,128)(2,1)} broadcast(bf16[24,5120]{1,0:T(8,128)(2,1)} %param.9), dimensions={1,2} | broadcast | bytes 2211840 | tf_op jit(solution)/shard_map/broadcast_in_dim | solution.py:336
  3.1 7.1 %all-to-all-start = ((bf16[8,24,5120]{2,1,0:T(8,128)(2,1)}), bf16[8,24,5120]{2,1,0:T(8,128)(2,1)}, u32[]{:S(2)}, u32[]{:S(2)}) async-start(bf16[8,24,5120]{2,1,0:T(8,128)(2,1)} %broadcast_in_dim.12), calls=%async_computation | async-start | bytes 3932160 | tf_op jit(solution)/shard_map/all_to_all | solution.py:335
  10.3 0.6 convert_reduce_fusion
  12.6 2.0 pad_maximum_fusion.w_ref
  14.6 20.7 %all-to-all-done = bf16[8,24,5120]{2,1,0:T(8,128)(2,1)} async-done(((bf16[8,24,5120]{2,1,0:T(8,128)(2,1)}), bf16[8,24,5120]{2,1,0:T(8,128)(2,1)}, u32[]{:S(2)}, u32[]{:S(2)}) %all-to-all-start) | async-done | bytes 1966112 | tf_op jit(solution)/shard_map/all_to_all | solution.py:335
  35.3 2.2 constant_dynamic-update-slice_fusion.5
  37.5 0.7 collective-permute-start
  38.2 4.0 %collective-permute-done = bf16[192,256]{1,0:T(8,128)(2,1)S(1)} collective-permute-done((bf16[192,256]{1,0:T(8,128)(2,1)S(1)}, bf16[192,256]{1,0:T(8,128)(2,1)S(1)}, u32[]{:S(2)}, u32[]{:S(2)}) %collective-permute-start) | collective-permute-done | bytes 98336 | tf_op jit(solution)/shard_map/ppermute | solution.py:341
  42.2 2.0 collective-permute-start.1
  44.4 3.6 %collective-permute-done.1 = bf16[2,192,256]{2,1,0:T(8,128)(2,1)S(1)} collective-permute-done((bf16[2,192,256]{2,1,0:T(8,128)(2,1)S(1)}, bf16[2,192,256]{2,1,0:T(8,128)(2,1)S(1)}, u32[]{:S(2)}, u32[]{:S(2)}) %collective-permute-start.1) | collective-permute-done | bytes 196640 | tf_op jit(solution)/shard_map/ppermute | solution.py:346
  48.0 2.3 %collective-permute-start.3 = (bf16[2,192,256]{2,1,0:T(8,128)(2,1)S(1)}, bf16[2,192,256]{2,1,0:T(8,128)(2,1)S(1)}, u32[]{:S(2)}, u32[]{:S(2)}) collective-permute-start(bf16[2,192,256]{2,1,0:T(8,128)(2,1)S(1)} %collective-permute-done.1), channel_id=1, source_target_pairs={{0,32},{32,64},{64,96},{96,128},{128,160},{160,192},{192,224},{224... | collective-permute-start | bytes 589832 | tf_op jit(solution)/shard_map/ppermute | solution.py:346
  50.3 1.7 collective-permute-start.4
  52.0 3.6 %collective-permute-done.3 = bf16[2,192,256]{2,1,0:T(8,128)(2,1)S(1)} collective-permute-done((bf16[2,192,256]{2,1,0:T(8,128)(2,1)S(1)}, bf16[2,192,256]{2,1,0:T(8,128)(2,1)S(1)}, u32[]{:S(2)}, u32[]{:S(2)}) %collective-permute-start.3) | collective-permute-done | bytes 196640 | tf_op jit(solution)/shard_map/ppermute | solution.py:346
  55.6 1.0 collective-permute-done.4
  56.7 3.3 %collective-permute-start.5 = (bf16[2,192,256]{2,1,0:T(8,128)(2,1)S(1)}, bf16[2,192,256]{2,1,0:T(8,128)(2,1)S(1)}, u32[]{:S(2)}, u32[]{:S(2)}) collective-permute-start(bf16[2,192,256]{2,1,0:T(8,128)(2,1)S(1)} %collective-permute-done.3), channel_id=1, source_target_pairs={{0,32},{32,64},{64,96},{96,128},{128,160},{160,192},{192,224},{224... | collective-permute-start | bytes 589832 | tf_op jit(solution)/shard_map/ppermute | solution.py:346
  60.0 4.7 %collective-permute-done.5 = bf16[2,192,256]{2,1,0:T(8,128)(2,1)S(1)} collective-permute-done((bf16[2,192,256]{2,1,0:T(8,128)(2,1)S(1)}, bf16[2,192,256]{2,1,0:T(8,128)(2,1)S(1)}, u32[]{:S(2)}, u32[]{:S(2)}) %collective-permute-start.5) | collective-permute-done | bytes 196640 | tf_op jit(solution)/shard_map/ppermute | solution.py:346
  64.8 3.2 %collective-permute-start.7 = (bf16[1,192,256]{2,1,0:T(8,128)(2,1)S(1)}, bf16[1,192,256]{2,1,0:T(8,128)(2,1)S(1)}, u32[]{:S(2)}, u32[]{:S(2)}) collective-permute-start(bf16[1,192,256]{2,1,0:T(8,128)(2,1)S(1)} %slice.65), channel_id=1, source_target_pairs={{0,32},{32,64},{64,96},{96,128},{128,160},{160,192},{192,224},{224... | collective-permute-start | bytes 294920 | tf_op jit(solution)/shard_map/ppermute | solution.py:349
  68.7 2.0 collective-permute-done.7
  70.7 2.5 %collective-permute-done.8 = bf16[1,192,256]{2,1,0:T(8,128)(2,1)S(1)} collective-permute-done((bf16[1,192,256]{2,1,0:T(8,128)(2,1)S(1)}, bf16[1,192,256]{2,1,0:T(8,128)(2,1)S(1)}, u32[]{:S(2)}, u32[]{:S(2)}) %collective-permute-start.8) | collective-permute-done | bytes 98336 | tf_op jit(solution)/shard_map/ppermute | solution.py:350
  73.5 1.4 collective-permute-done.11.refs_5_
  75.0 10.8 %attention.1 = (bf16[192,640]{1,0:T(8,128)(2,1)}, bf16[192,640]{1,0:T(8,128)(2,1)}, bf16[16,96,256]{2,1,0:T(8,128)(2,1)S(1)}, bf16[8,96,256]{2,1,0:T(8,128)(2,1)...) custom-call(s32[136]{0:T(256)S(1)} %pad_add_fusion.2.table_ref, ...), custom_call_target="tpu_custom_call" | custom-call | tf_op jit(solution)/shard_map/attention/pallas_call | solution.py:161
  85.8 3.5 %collective-permute-start.13 = (bf16[8,96,256]{2,1,0:T(8,128)(2,1)S(1)}, bf16[8,96,256]{2,1,0:T(8,128)(2,1)S(1)}, u32[]{:S(2)}, u32[]{:S(2)}) collective-permute-start(bf16[8,96,256]{2,1,0:T(8,128)(2,1)S(1)} %get-tuple-element.38), channel_id=1, source_target_pairs={{0,8},{8,0},{1,9},{9,1},{2,10},{10,2},{3,11},{11,3},{4,12},{12,4},... | collective-permute-start | bytes 1179656 | tf_op jit(solution)/shard_map/ppermute | solution.py:366
  89.8 0.8 collective-permute-done.13
  90.7 0.9 add_convert_fusion.1
  91.6 3.0 %collective-permute-start.14 = (bf16[8,96,256]{2,1,0:T(8,128)(2,1)}, bf16[8,96,256]{2,1,0:T(8,128)(2,1)}, u32[]{:S(2)}, u32[]{:S(2)}) collective-permute-start(bf16[8,96,256]{2,1,0:T(8,128)(2,1)} %add_convert_fusion.1), channel_id=1, source_target_pairs={{0,16},{16,0},{1,17},{17,1},{2,18},{18,2},{3,19},{19,3},{4,20},{20... | collective-permute-start | bytes 1179656 | tf_op jit(solution)/shard_map/ppermute | solution.py:369
  94.6 0.8 add_convert_fusion
  95.4 11.8 %all-to-all-start.1 = ((bf16[8,96,256]{2,1,0:T(8,128)(2,1)}), bf16[8,96,256]{2,1,0:T(8,128)(2,1)}, u32[]{:S(2)}, u32[]{:S(2)}) async-start(bf16[8,96,256]{2,1,0:T(8,128)(2,1)} %add_convert_fusion), calls=%async_computation.1 | async-start | bytes 786432 | tf_op jit(solution)/shard_map/all_to_all | solution.py:370
  107.2 1.3 convert_add_fusion
  108.6 2.4 %fusion.21 = (bf16[8,2,96,256]{3,2,0,1:T(8,128)(2,1)S(1)}, f32[8,2,96,256]{3,2,0,1:T(8,128)}) fusion(bf16[8,1,96,256]{3,2,0,1:T(8,128)(2,1)} %bitcast.8, f32[8,2,96,256]{3,2,1,0:T(8,128)S(1)} %bitcast.84), kind=kLoop, calls=%fused_computation.77 | loop fusion | flops 1179648 | bytes 4325376 | tf_op jit(solution)/shard_map/convert.13
  111.0 0.7 slice_bitcast_fusion.7
  111.7 4.5 %collective-permute-start.15 = (bf16[2,96,256]{2,1,0:T(8,128)(2,1)S(1)}, bf16[2,96,256]{2,1,0:T(8,128)(2,1)S(1)}, u32[]{:S(2)}, u32[]{:S(2)}) collective-permute-start(bf16[2,96,256]{2,1,0:T(8,128)(2,1)S(1)} %get-tuple-element.60), channel_id=1, source_target_pairs={{0,128},{32,160},{64,192},{96,224},{128,0},{160,32},{192,64},{224,... | collective-permute-start | bytes 294920 | tf_op jit(solution)/shard_map/ppermute | solution.py:377
  116.2 1.5 collective-permute-start.16
  117.6 3.6 %collective-permute-start.17 = (bf16[2,96,256]{2,1,0:T(8,128)(2,1)}, bf16[2,96,256]{2,1,0:T(8,128)(2,1)S(1)}, u32[]{:S(2)}, u32[]{:S(2)}) collective-permute-start(bf16[2,96,256]{2,1,0:T(8,128)(2,1)} %get-tuple-element.63), channel_id=1, source_target_pairs={{0,96},{32,128},{64,160},{96,192},{128,224},{160,0},{192,32},{224,... | collective-permute-start | bytes 294920 | tf_op jit(solution)/shard_map/ppermute | solution.py:377
  121.2 2.4 %collective-permute-start.18 = (bf16[2,96,256]{2,1,0:T(8,128)(2,1)S(1)}, bf16[2,96,256]{2,1,0:T(8,128)(2,1)S(1)}, u32[]{:S(2)}, u32[]{:S(2)}) collective-permute-start(bf16[2,96,256]{2,1,0:T(8,128)(2,1)S(1)} %get-tuple-element.62), channel_id=1, source_target_pairs={{0,192},{32,224},{64,0},{96,32},{128,64},{160,96},{192,128},{224,1... | collective-permute-start | bytes 294920 | tf_op jit(solution)/shard_map/ppermute | solution.py:377
  123.6 2.4 %collective-permute-start.19 = (bf16[2,96,256]{2,1,0:T(8,128)(2,1)S(1)}, bf16[2,96,256]{2,1,0:T(8,128)(2,1)S(1)}, u32[]{:S(2)}, u32[]{:S(2)}) collective-permute-start(bf16[2,96,256]{2,1,0:T(8,128)(2,1)S(1)} %get-tuple-element.61), channel_id=1, source_target_pairs={{0,64},{32,96},{64,128},{96,160},{128,192},{160,224},{192,0},{224,... | collective-permute-start | bytes 294920 | tf_op jit(solution)/shard_map/ppermute | solution.py:377
  125.9 2.1 collective-permute-start.20
  128.0 3.0 %collective-permute-done.16 = bf16[2,96,256]{2,1,0:T(8,128)(2,1)S(1)} collective-permute-done((bf16[2,96,256]{2,1,0:T(8,128)(2,1)S(1)}, bf16[2,96,256]{2,1,0:T(8,128)(2,1)S(1)}, u32[]{:S(2)}, u32[]{:S(2)}) %collective-permute-start.16) | collective-permute-done | bytes 98336 | tf_op jit(solution)/shard_map/ppermute | solution.py:377
  131.0 1.7 reduce_sum.32
  132.7 1.8 collective-permute-start.23
  134.5 1.5 collective-permute-done.18
  136.0 1.7 collective-permute-done.20
  137.9 1.1 fusion.8
  139.0 1.0 grad_rows.1
  140.0 1.3 copy-done
  141.3 5.4 %all-to-all-start.2 = ((bf16[8,24,5120]{2,1,0:T(8,128)(2,1)}), bf16[8,24,5120]{2,1,0:T(8,128)(2,1)S(1)}, u32[]{:S(2)}, u32[]{:S(2)}) async-start(bf16[8,24,5120]{2,1,0:T(8,128)(2,1)} %bitcast.79), calls=%async_computation.2 | async-start | bytes 3932160 | tf_op jit(solution)/shard_map/all_to_all | solution.py:387
  146.7 2.5 %strips.1 = (bf16[8,160,192]{2,1,0:T(8,128)(2,1)S(1)}, bf16[8,160,192]{2,1,0:T(8,128)(2,1)S(1)}, bf16[8,160,192]{2,1,0:T(8,128)(2,1)S(1)}, bf16[8,160,192]{2,1,0:T(8,128)(2,1)S(1)}) custom-call(s32[4]{0:T(128)S(1)} %pad_add_fusion.3.at_ref, bf16[192,5120]{1,0:T(8,128)(2,1)} %bitcast.rows_ref), custom_call_target="tpu_custom_call" | custom-call | tf_op jit(solution)/shard_map/strips/pallas_call | solution.py:193
  150.1 1.3 collective-permute-done.26
  151.9 1.6 collective-permute-start.29
  153.5 45.0 %collective-permute-done.29.refs_6_ = bf16[192,256]{1,0:T(8,128)(2,1)S(1)} collective-permute-done((bf16[192,256]{1,0:T(8,128)(2,1)S(1)}, bf16[192,256]{1,0:T(8,128)(2,1)S(1)}, u32[]{:S(2)}, u32[]{:S(2)}) %collective-permute-start.29) | collective-permute-done | bytes 98336 | tf_op jit(solution)/shard_map/ppermute | solution.py:383
  198.5 1.3 collective-permute-done.30.refs_7_
  199.7 0.8 grad_w.1
  200.6 3.3 %collective-permute-start.31 = (bf16[160,256]{1,0:T(8,128)(2,1)S(1)}, bf16[160,256]{1,0:T(8,128)(2,1)S(1)}, u32[]{:S(2)}, u32[]{:S(2)}) collective-permute-start(bf16[160,256]{1,0:T(8,128)(2,1)S(1)} %get-tuple-element.46), channel_id=1, source_target_pairs={{0,128},{32,160},{64,192},{96,224},{128,0},{160,32},{192,64},{224,... | collective-permute-start | bytes 245768 | tf_op jit(solution)/shard_map/ppermute | solution.py:393
  203.8 2.9 %collective-permute-start.32 = (bf16[160,256]{1,0:T(8,128)(2,1)S(1)}, bf16[160,256]{1,0:T(8,128)(2,1)S(1)}, u32[]{:S(2)}, u32[]{:S(2)}) collective-permute-start(bf16[160,256]{1,0:T(8,128)(2,1)S(1)} %get-tuple-element.47), channel_id=1, source_target_pairs={{0,96},{32,128},{64,160},{96,192},{128,224},{160,0},{192,32},{224,... | collective-permute-start | bytes 245768 | tf_op jit(solution)/shard_map/ppermute | solution.py:393
  206.7 2.2 collective-permute-start.33
  208.9 1.6 collective-permute-start.34
  210.5 2.5 %collective-permute-start.35 = (bf16[160,256]{1,0:T(8,128)(2,1)S(1)}, bf16[160,256]{1,0:T(8,128)(2,1)S(1)}, u32[]{:S(2)}, u32[]{:S(2)}) collective-permute-start(bf16[160,256]{1,0:T(8,128)(2,1)S(1)} %get-tuple-element.50), channel_id=1, source_target_pairs={{0,192},{32,224},{64,0},{96,32},{128,64},{160,96},{192,128},{224,1... | collective-permute-start | bytes 245768 | tf_op jit(solution)/shard_map/ppermute | solution.py:393
  213.0 2.8 %collective-permute-start.36 = (bf16[160,256]{1,0:T(8,128)(2,1)S(1)}, bf16[160,256]{1,0:T(8,128)(2,1)S(1)}, u32[]{:S(2)}, u32[]{:S(2)}) collective-permute-start(bf16[160,256]{1,0:T(8,128)(2,1)S(1)} %get-tuple-element.51), channel_id=1, source_target_pairs={{0,32},{32,64},{64,96},{96,128},{128,160},{160,192},{192,224},{224... | collective-permute-start | bytes 245768 | tf_op jit(solution)/shard_map/ppermute | solution.py:393
  215.9 2.0 collective-permute-done.32
  217.9 0.6 collective-permute-start.37
  218.5 1.8 collective-permute-done.34
  220.3 0.6 collective-permute-done.36
  220.9 1.5 collective-permute-done.37
  222.4 0.7 fusion.24
  223.1 0.9 total.1
  (97 shorter events, 5.2 us)
Async XLA Ops:
  3.1 7.1 %copy-start.6 = (s32[64]{0:T(128)S(1)}, s32[64]{0:T(128)}, u32[]{:S(2)}) copy-start(s32[64]{0:T(128)} %param.14) | copy-start | bytes 772
  3.1 7.2 %copy-start.3 = (s32[6144]{0:T(1024)S(1)}, s32[6144]{0:T(1024)}, u32[]{:S(2)}) copy-start(s32[6144]{0:T(1024)} %param.15) | copy-start | bytes 73732
  3.1 8.3 %copy-start.4 = (s32[16]{0:T(128)S(1)}, s32[16]{0:T(128)}, u32[]{:S(2)}) copy-start(s32[16]{0:T(128)} %constant.106.clone) | copy-start | bytes 196
  3.1 8.3 %copy-start.5 = (s32[16]{0:T(128)S(1)}, s32[16]{0:T(128)}, u32[]{:S(2)}) copy-start(s32[16]{0:T(128)} %constant.116) | copy-start | bytes 196
  3.1 32.2 %all-to-all-start = ((bf16[8,24,5120]{2,1,0:T(8,128)(2,1)}), bf16[8,24,5120]{2,1,0:T(8,128)(2,1)}, u32[]{:S(2)}, u32[]{:S(2)}) async-start(bf16[8,24,5120]{2,1,0:T(8,128)(2,1)} %broadcast_in_dim.12), calls=%async_computation | async-start | bytes 3932160 | tf_op jit(solution)/shard_map/all_to_all | solution.py:335
  37.5 37.5 %copy-start.1 = (bf16[192,640]{1,0:T(8,128)(2,1)S(1)}, bf16[192,640]{1,0:T(8,128)(2,1)}, u32[]{:S(2)}) copy-start(bf16[192,640]{1,0:T(8,128)(2,1)} %q_ref.1) | copy-start | bytes 737284
  37.5 37.5 %copy-start.2 = (bf16[192,640]{1,0:T(8,128)(2,1)S(1)}, bf16[192,640]{1,0:T(8,128)(2,1)}, u32[]{:S(2)}) copy-start(bf16[192,640]{1,0:T(8,128)(2,1)} %g_ref.1) | copy-start | bytes 737284
  37.5 4.7 %collective-permute-start = (bf16[192,256]{1,0:T(8,128)(2,1)S(1)}, bf16[192,256]{1,0:T(8,128)(2,1)S(1)}, u32[]{:S(2)}, u32[]{:S(2)}) collective-permute-start(bf16[192,256]{1,0:T(8,128)(2,1)S(1)} %get-tuple-element.72), channel_id=1, source_target_pairs={{0,16},{16,0},{1,17},{17,1},{2,18},{18,2},{3,19},{19,3},{4,20},{20... | collective-permute-start | bytes 294920 | tf_op jit(solution)/shard_map/ppermute | solution.py:341
  42.2 5.7 %collective-permute-start.1 = (bf16[2,192,256]{2,1,0:T(8,128)(2,1)S(1)}, bf16[2,192,256]{2,1,0:T(8,128)(2,1)S(1)}, u32[]{:S(2)}, u32[]{:S(2)}) collective-permute-start(bf16[2,192,256]{2,1,0:T(8,128)(2,1)S(1)} %pad_maximum_fusion.1), channel_id=1, source_target_pairs={{0,32},{32,64},{64,96},{96,128},{128,160},{160,192},{192,224},{224... | collective-permute-start | bytes 589832 | tf_op jit(solution)/shard_map/ppermute | solution.py:346
  44.2 6.0 %collective-permute-start.2 = (bf16[2,192,256]{2,1,0:T(8,128)(2,1)S(1)}, bf16[2,192,256]{2,1,0:T(8,128)(2,1)S(1)}, u32[]{:S(2)}, u32[]{:S(2)}) collective-permute-start(bf16[2,192,256]{2,1,0:T(8,128)(2,1)S(1)} %pad_maximum_fusion.1), channel_id=1, source_target_pairs={{0,224},{32,0},{64,32},{96,64},{128,96},{160,128},{192,160},{224,1... | collective-permute-start | bytes 589832 | tf_op jit(solution)/shard_map/ppermute | solution.py:347
  48.0 7.6 %collective-permute-start.3 = (bf16[2,192,256]{2,1,0:T(8,128)(2,1)S(1)}, bf16[2,192,256]{2,1,0:T(8,128)(2,1)S(1)}, u32[]{:S(2)}, u32[]{:S(2)}) collective-permute-start(bf16[2,192,256]{2,1,0:T(8,128)(2,1)S(1)} %collective-permute-done.1), channel_id=1, source_target_pairs={{0,32},{32,64},{64,96},{96,128},{128,160},{160,192},{192,224},{224... | collective-permute-start | bytes 589832 | tf_op jit(solution)/shard_map/ppermute | solution.py:346
  50.3 6.3 %collective-permute-start.4 = (bf16[2,192,256]{2,1,0:T(8,128)(2,1)S(1)}, bf16[2,192,256]{2,1,0:T(8,128)(2,1)S(1)}, u32[]{:S(2)}, u32[]{:S(2)}) collective-permute-start(bf16[2,192,256]{2,1,0:T(8,128)(2,1)S(1)} %collective-permute-done.2), channel_id=1, source_target_pairs={{0,224},{32,0},{64,32},{96,64},{128,96},{160,128},{192,160},{224,1... | collective-permute-start | bytes 589832 | tf_op jit(solution)/shard_map/ppermute | solution.py:347
  56.6 18.4 %collective-permute-start.9 = (bf16[10,192,256]{2,1,0:T(8,128)(2,1)S(1)}, bf16[10,192,256]{2,1,0:T(8,128)(2,1)S(1)}, u32[]{:S(2)}, u32[]{:S(2)}) collective-permute-start(bf16[10,192,256]{2,1,0:T(8,128)(2,1)S(1)} %constant_dynamic-update-slice_fusion.refs_0_), channel_id=1, source_target_pairs={{0,8},{8,0},{1,9},{9,1},{2,10},{10,2},{3,11},{11,3},{4,12},{12,4},... | collective-permute-start | bytes 2949128 | tf_op jit(solution)/shard_map/ppermute | solution.py:354
  56.7 8.1 %collective-permute-start.5 = (bf16[2,192,256]{2,1,0:T(8,128)(2,1)S(1)}, bf16[2,192,256]{2,1,0:T(8,128)(2,1)S(1)}, u32[]{:S(2)}, u32[]{:S(2)}) collective-permute-start(bf16[2,192,256]{2,1,0:T(8,128)(2,1)S(1)} %collective-permute-done.3), channel_id=1, source_target_pairs={{0,32},{32,64},{64,96},{96,128},{128,160},{160,192},{192,224},{224... | collective-permute-start | bytes 589832 | tf_op jit(solution)/shard_map/ppermute | solution.py:346
  60.0 8.4 %collective-permute-start.6 = (bf16[2,192,256]{2,1,0:T(8,128)(2,1)S(1)}, bf16[2,192,256]{2,1,0:T(8,128)(2,1)S(1)}, u32[]{:S(2)}, u32[]{:S(2)}) collective-permute-start(bf16[2,192,256]{2,1,0:T(8,128)(2,1)S(1)} %collective-permute-done.4), channel_id=1, source_target_pairs={{0,224},{32,0},{64,32},{96,64},{128,96},{160,128},{192,160},{224,1... | collective-permute-start | bytes 589832 | tf_op jit(solution)/shard_map/ppermute | solution.py:347
  64.8 5.9 %collective-permute-start.7 = (bf16[1,192,256]{2,1,0:T(8,128)(2,1)S(1)}, bf16[1,192,256]{2,1,0:T(8,128)(2,1)S(1)}, u32[]{:S(2)}, u32[]{:S(2)}) collective-permute-start(bf16[1,192,256]{2,1,0:T(8,128)(2,1)S(1)} %slice.65), channel_id=1, source_target_pairs={{0,32},{32,64},{64,96},{96,128},{128,160},{160,192},{192,224},{224... | collective-permute-start | bytes 294920 | tf_op jit(solution)/shard_map/ppermute | solution.py:349
  68.5 4.8 %collective-permute-start.8 = (bf16[1,192,256]{2,1,0:T(8,128)(2,1)S(1)}, bf16[1,192,256]{2,1,0:T(8,128)(2,1)S(1)}, u32[]{:S(2)}, u32[]{:S(2)}) collective-permute-start(bf16[1,192,256]{2,1,0:T(8,128)(2,1)S(1)} %slice.66), channel_id=1, source_target_pairs={{0,224},{32,0},{64,32},{96,64},{128,96},{160,128},{192,160},{224,1... | collective-permute-start | bytes 294920 | tf_op jit(solution)/shard_map/ppermute | solution.py:350
  68.6 6.4 %collective-permute-start.10 = (bf16[4,192,256]{2,1,0:T(8,128)(2,1)S(1)}, bf16[4,192,256]{2,1,0:T(8,128)(2,1)S(1)}, u32[]{:S(2)}, u32[]{:S(2)}) collective-permute-start(bf16[4,192,256]{2,1,0:T(8,128)(2,1)S(1)} %constant_dynamic-update-slice_fusion.6.refs_1_), channel_id=1, source_target_pairs={{0,8},{8,0},{1,9},{9,1},{2,10},{10,2},{3,11},{11,3},{4,12},{12,4},... | collective-permute-start | bytes 1179656 | tf_op jit(solution)/shard_map/ppermute | solution.py:354
  73.3 1.7 collective-permute-start.11
  85.8 4.9 %collective-permute-start.13 = (bf16[8,96,256]{2,1,0:T(8,128)(2,1)S(1)}, bf16[8,96,256]{2,1,0:T(8,128)(2,1)S(1)}, u32[]{:S(2)}, u32[]{:S(2)}) collective-permute-start(bf16[8,96,256]{2,1,0:T(8,128)(2,1)S(1)} %get-tuple-element.38), channel_id=1, source_target_pairs={{0,8},{8,0},{1,9},{9,1},{2,10},{10,2},{3,11},{11,3},{4,12},{12,4},... | collective-permute-start | bytes 1179656 | tf_op jit(solution)/shard_map/ppermute | solution.py:366
  89.3 17.9 %collective-permute-start.12 = (bf16[16,96,256]{2,1,0:T(8,128)(2,1)}, bf16[16,96,256]{2,1,0:T(8,128)(2,1)}, u32[]{:S(2)}, u32[]{:S(2)}) collective-permute-start(bf16[16,96,256]{2,1,0:T(8,128)(2,1)} %get-tuple-element.36), channel_id=1, source_target_pairs={{0,8},{8,0},{1,9},{9,1},{2,10},{10,2},{3,11},{11,3},{4,12},{12,4},... | collective-permute-start | bytes 2359304 | tf_op jit(solution)/shard_map/ppermute | solution.py:368
  89.3 5.2 %collective-permute-start.22 = (bf16[8,96,256]{2,1,0:T(8,128)(2,1)S(1)}, bf16[8,96,256]{2,1,0:T(8,128)(2,1)S(1)}, u32[]{:S(2)}, u32[]{:S(2)}) collective-permute-start(bf16[8,96,256]{2,1,0:T(8,128)(2,1)S(1)} %get-tuple-element.40), channel_id=1, source_target_pairs={{0,8},{8,0},{1,9},{9,1},{2,10},{10,2},{3,11},{11,3},{4,12},{12,4},... | collective-permute-start | bytes 1179656 | tf_op jit(solution)/shard_map/ppermute | solution.py:367
  91.6 17.0 %collective-permute-start.14 = (bf16[8,96,256]{2,1,0:T(8,128)(2,1)}, bf16[8,96,256]{2,1,0:T(8,128)(2,1)}, u32[]{:S(2)}, u32[]{:S(2)}) collective-permute-start(bf16[8,96,256]{2,1,0:T(8,128)(2,1)} %add_convert_fusion.1), channel_id=1, source_target_pairs={{0,16},{16,0},{1,17},{17,1},{2,18},{18,2},{3,19},{19,3},{4,20},{20... | collective-permute-start | bytes 1179656 | tf_op jit(solution)/shard_map/ppermute | solution.py:369
  95.4 35.6 %all-to-all-start.1 = ((bf16[8,96,256]{2,1,0:T(8,128)(2,1)}), bf16[8,96,256]{2,1,0:T(8,128)(2,1)}, u32[]{:S(2)}, u32[]{:S(2)}) async-start(bf16[8,96,256]{2,1,0:T(8,128)(2,1)} %add_convert_fusion), calls=%async_computation.1 | async-start | bytes 786432 | tf_op jit(solution)/shard_map/all_to_all | solution.py:370
  111.7 14.2 %collective-permute-start.15 = (bf16[2,96,256]{2,1,0:T(8,128)(2,1)S(1)}, bf16[2,96,256]{2,1,0:T(8,128)(2,1)S(1)}, u32[]{:S(2)}, u32[]{:S(2)}) collective-permute-start(bf16[2,96,256]{2,1,0:T(8,128)(2,1)S(1)} %get-tuple-element.60), channel_id=1, source_target_pairs={{0,128},{32,160},{64,192},{96,224},{128,0},{160,32},{192,64},{224,... | collective-permute-start | bytes 294920 | tf_op jit(solution)/shard_map/ppermute | solution.py:377
  116.2 14.8 %collective-permute-start.16 = (bf16[2,96,256]{2,1,0:T(8,128)(2,1)S(1)}, bf16[2,96,256]{2,1,0:T(8,128)(2,1)S(1)}, u32[]{:S(2)}, u32[]{:S(2)}) collective-permute-start(bf16[2,96,256]{2,1,0:T(8,128)(2,1)S(1)} %get-tuple-element.64), channel_id=1, source_target_pairs={{0,160},{32,192},{64,224},{96,0},{128,32},{160,64},{192,96},{224,1... | collective-permute-start | bytes 294920 | tf_op jit(solution)/shard_map/ppermute | solution.py:377
  117.6 15.1 %collective-permute-start.17 = (bf16[2,96,256]{2,1,0:T(8,128)(2,1)}, bf16[2,96,256]{2,1,0:T(8,128)(2,1)S(1)}, u32[]{:S(2)}, u32[]{:S(2)}) collective-permute-start(bf16[2,96,256]{2,1,0:T(8,128)(2,1)} %get-tuple-element.63), channel_id=1, source_target_pairs={{0,96},{32,128},{64,160},{96,192},{128,224},{160,0},{192,32},{224,... | collective-permute-start | bytes 294920 | tf_op jit(solution)/shard_map/ppermute | solution.py:377
  121.2 14.8 %collective-permute-start.18 = (bf16[2,96,256]{2,1,0:T(8,128)(2,1)S(1)}, bf16[2,96,256]{2,1,0:T(8,128)(2,1)S(1)}, u32[]{:S(2)}, u32[]{:S(2)}) collective-permute-start(bf16[2,96,256]{2,1,0:T(8,128)(2,1)S(1)} %get-tuple-element.62), channel_id=1, source_target_pairs={{0,192},{32,224},{64,0},{96,32},{128,64},{160,96},{192,128},{224,1... | collective-permute-start | bytes 294920 | tf_op jit(solution)/shard_map/ppermute | solution.py:377
  123.6 12.4 %collective-permute-start.19 = (bf16[2,96,256]{2,1,0:T(8,128)(2,1)S(1)}, bf16[2,96,256]{2,1,0:T(8,128)(2,1)S(1)}, u32[]{:S(2)}, u32[]{:S(2)}) collective-permute-start(bf16[2,96,256]{2,1,0:T(8,128)(2,1)S(1)} %get-tuple-element.61), channel_id=1, source_target_pairs={{0,64},{32,96},{64,128},{96,160},{128,192},{160,224},{192,0},{224,... | collective-permute-start | bytes 294920 | tf_op jit(solution)/shard_map/ppermute | solution.py:377
  125.9 11.7 %collective-permute-start.20 = (bf16[2,96,256]{2,1,0:T(8,128)(2,1)S(1)}, bf16[2,96,256]{2,1,0:T(8,128)(2,1)}, u32[]{:S(2)}, u32[]{:S(2)}) collective-permute-start(bf16[2,96,256]{2,1,0:T(8,128)(2,1)S(1)} %get-tuple-element.66), channel_id=1, source_target_pairs={{0,224},{32,0},{64,32},{96,64},{128,96},{160,128},{192,160},{224,1... | collective-permute-start | bytes 294920 | tf_op jit(solution)/shard_map/ppermute | solution.py:377
  131.0 6.9 %collective-permute-start.21 = (bf16[2,96,256]{2,1,0:T(8,128)(2,1)S(1)}, bf16[2,96,256]{2,1,0:T(8,128)(2,1)}, u32[]{:S(2)}, u32[]{:S(2)}) collective-permute-start(bf16[2,96,256]{2,1,0:T(8,128)(2,1)S(1)} %get-tuple-element.65), channel_id=1, source_target_pairs={{0,32},{32,64},{64,96},{96,128},{128,160},{160,192},{192,224},{224... | collective-permute-start | bytes 294920 | tf_op jit(solution)/shard_map/ppermute | solution.py:377
  132.7 5.2 %collective-permute-start.23 = (bf16[96,256]{1,0:T(8,128)(2,1)}, bf16[96,256]{1,0:T(8,128)(2,1)S(1)}, u32[]{:S(2)}, u32[]{:S(2)}) collective-permute-start(bf16[96,256]{1,0:T(8,128)(2,1)} %reduce_sum.32), channel_id=1, source_target_pairs={{0,16},{16,0},{1,17},{17,1},{2,18},{18,2},{3,19},{19,3},{4,20},{20... | collective-permute-start | bytes 147464 | tf_op jit(solution)/shard_map/ppermute | solution.py:379
  140.0 1.3 copy-start
  141.3 81.8 %all-to-all-start.2 = ((bf16[8,24,5120]{2,1,0:T(8,128)(2,1)}), bf16[8,24,5120]{2,1,0:T(8,128)(2,1)S(1)}, u32[]{:S(2)}, u32[]{:S(2)}) async-start(bf16[8,24,5120]{2,1,0:T(8,128)(2,1)} %bitcast.79), calls=%async_computation.2 | async-start | bytes 3932160 | tf_op jit(solution)/shard_map/all_to_all | solution.py:387
  149.2 2.2 collective-permute-start.26
  149.3 49.1 %collective-permute-start.24 = (bf16[8,160,192]{2,1,0:T(8,128)(2,1)S(1)}, bf16[8,160,192]{2,1,0:T(8,128)(2,1)S(1)}, u32[]{:S(2)}, u32[]{:S(2)}) collective-permute-start(bf16[8,160,192]{2,1,0:T(8,128)(2,1)S(1)} %get-tuple-element.42), channel_id=1, source_target_pairs={{0,8},{8,0},{1,9},{9,1},{2,10},{10,2},{3,11},{11,3},{4,12},{12,4},... | collective-permute-start | bytes 1474568 | tf_op jit(solution)/shard_map/ppermute | solution.py:359
  149.8 48.6 %collective-permute-start.25 = (bf16[8,160,192]{2,1,0:T(8,128)(2,1)S(1)}, bf16[8,160,192]{2,1,0:T(8,128)(2,1)S(1)}, u32[]{:S(2)}, u32[]{:S(2)}) collective-permute-start(bf16[8,160,192]{2,1,0:T(8,128)(2,1)S(1)} %get-tuple-element.43), channel_id=1, source_target_pairs={{0,16},{16,0},{1,17},{17,1},{2,18},{18,2},{3,19},{19,3},{4,20},{20... | collective-permute-start | bytes 1474568 | tf_op jit(solution)/shard_map/ppermute | solution.py:358
  151.4 47.0 %collective-permute-start.27 = (bf16[8,160,192]{2,1,0:T(8,128)(2,1)S(1)}, bf16[8,160,192]{2,1,0:T(8,128)(2,1)S(1)}, u32[]{:S(2)}, u32[]{:S(2)}) collective-permute-start(bf16[8,160,192]{2,1,0:T(8,128)(2,1)S(1)} %collective-permute-done.26), channel_id=1, source_target_pairs={{0,16},{16,0},{1,17},{17,1},{2,18},{18,2},{3,19},{19,3},{4,20},{20... | collective-permute-start | bytes 1474568 | tf_op jit(solution)/shard_map/ppermute | solution.py:360
  151.9 46.6 %collective-permute-start.29 = (bf16[192,256]{1,0:T(8,128)(2,1)S(1)}, bf16[192,256]{1,0:T(8,128)(2,1)S(1)}, u32[]{:S(2)}, u32[]{:S(2)}) collective-permute-start(bf16[192,256]{1,0:T(8,128)(2,1)S(1)} %bitcast.81), channel_id=1, source_target_pairs={{0,16},{16,0},{1,17},{17,1},{2,18},{18,2},{3,19},{19,3},{4,20},{20... | collective-permute-start | bytes 294920 | tf_op jit(solution)/shard_map/ppermute | solution.py:383
  153.5 45.0 %collective-permute-start.28 = (bf16[192,256]{1,0:T(8,128)(2,1)S(1)}, bf16[192,256]{1,0:T(8,128)(2,1)S(1)}, u32[]{:S(2)}, u32[]{:S(2)}) collective-permute-start(bf16[192,256]{1,0:T(8,128)(2,1)S(1)} %bitcast.82), channel_id=1, source_target_pairs={{0,8},{8,0},{1,9},{9,1},{2,10},{10,2},{3,11},{11,3},{4,12},{12,4},... | collective-permute-start | bytes 294920 | tf_op jit(solution)/shard_map/ppermute | solution.py:384
  198.4 1.3 collective-permute-start.30
  200.6 12.4 %collective-permute-start.31 = (bf16[160,256]{1,0:T(8,128)(2,1)S(1)}, bf16[160,256]{1,0:T(8,128)(2,1)S(1)}, u32[]{:S(2)}, u32[]{:S(2)}) collective-permute-start(bf16[160,256]{1,0:T(8,128)(2,1)S(1)} %get-tuple-element.46), channel_id=1, source_target_pairs={{0,128},{32,160},{64,192},{96,224},{128,0},{160,32},{192,64},{224,... | collective-permute-start | bytes 245768 | tf_op jit(solution)/shard_map/ppermute | solution.py:393
  203.8 14.1 %collective-permute-start.32 = (bf16[160,256]{1,0:T(8,128)(2,1)S(1)}, bf16[160,256]{1,0:T(8,128)(2,1)S(1)}, u32[]{:S(2)}, u32[]{:S(2)}) collective-permute-start(bf16[160,256]{1,0:T(8,128)(2,1)S(1)} %get-tuple-element.47), channel_id=1, source_target_pairs={{0,96},{32,128},{64,160},{96,192},{128,224},{160,0},{192,32},{224,... | collective-permute-start | bytes 245768 | tf_op jit(solution)/shard_map/ppermute | solution.py:393
  206.7 11.8 %collective-permute-start.33 = (bf16[160,256]{1,0:T(8,128)(2,1)S(1)}, bf16[160,256]{1,0:T(8,128)(2,1)S(1)}, u32[]{:S(2)}, u32[]{:S(2)}) collective-permute-start(bf16[160,256]{1,0:T(8,128)(2,1)S(1)} %get-tuple-element.48), channel_id=1, source_target_pairs={{0,160},{32,192},{64,224},{96,0},{128,32},{160,64},{192,96},{224,1... | collective-permute-start | bytes 245768 | tf_op jit(solution)/shard_map/ppermute | solution.py:393
  208.9 11.4 %collective-permute-start.34 = (bf16[160,256]{1,0:T(8,128)(2,1)S(1)}, bf16[160,256]{1,0:T(8,128)(2,1)S(1)}, u32[]{:S(2)}, u32[]{:S(2)}) collective-permute-start(bf16[160,256]{1,0:T(8,128)(2,1)S(1)} %get-tuple-element.49), channel_id=1, source_target_pairs={{0,64},{32,96},{64,128},{96,160},{128,192},{160,224},{192,0},{224,... | collective-permute-start | bytes 245768 | tf_op jit(solution)/shard_map/ppermute | solution.py:393
  210.5 9.8 %collective-permute-start.35 = (bf16[160,256]{1,0:T(8,128)(2,1)S(1)}, bf16[160,256]{1,0:T(8,128)(2,1)S(1)}, u32[]{:S(2)}, u32[]{:S(2)}) collective-permute-start(bf16[160,256]{1,0:T(8,128)(2,1)S(1)} %get-tuple-element.50), channel_id=1, source_target_pairs={{0,192},{32,224},{64,0},{96,32},{128,64},{160,96},{192,128},{224,1... | collective-permute-start | bytes 245768 | tf_op jit(solution)/shard_map/ppermute | solution.py:393
  213.0 7.9 %collective-permute-start.36 = (bf16[160,256]{1,0:T(8,128)(2,1)S(1)}, bf16[160,256]{1,0:T(8,128)(2,1)S(1)}, u32[]{:S(2)}, u32[]{:S(2)}) collective-permute-start(bf16[160,256]{1,0:T(8,128)(2,1)S(1)} %get-tuple-element.51), channel_id=1, source_target_pairs={{0,32},{32,64},{64,96},{96,128},{128,160},{160,192},{192,224},{224... | collective-permute-start | bytes 245768 | tf_op jit(solution)/shard_map/ppermute | solution.py:393
  217.9 4.4 %collective-permute-start.37 = (bf16[160,256]{1,0:T(8,128)(2,1)S(1)}, bf16[160,256]{1,0:T(8,128)(2,1)S(1)}, u32[]{:S(2)}, u32[]{:S(2)}) collective-permute-start(bf16[160,256]{1,0:T(8,128)(2,1)S(1)} %get-tuple-element.52), channel_id=1, source_target_pairs={{0,224},{32,0},{64,32},{96,64},{128,96},{160,128},{192,160},{224,1... | collective-permute-start | bytes 245768 | tf_op jit(solution)/shard_map/ppermute | solution.py:393

commit v2 on v1

--- a/solution.py
+++ b/solution.py
@@ -46,13 +46,13 @@
                 kv_s[span_at(entry), :] = ref[j, i * SPAN : (i + 1) * SPAN]
                 entry += 1
 
-    def clear(p, carry):
-        acc_s[pl.ds(pl.multiple_of(p * SPAN, SPAN), SPAN), :] = jnp.zeros(
-            (SPAN, 2 * HEAD), jnp.float32
+    def clear(b, carry):
+        acc_s[pl.ds(pl.multiple_of(b * BLOCK, BLOCK), BLOCK), :] = jnp.zeros(
+            (BLOCK, 2 * HEAD), jnp.float32
         )
         return carry
 
-    lax.fori_loop(0, n_spans, clear, 0)
+    lax.fori_loop(0, n_spans // GROUP, clear, 0)
     qs[rows:, :] = jnp.zeros((wide - rows, HEAD), qs.dtype)
     gs[rows:, :] = jnp.zeros((wide - rows, HEAD), gs.dtype)
 

time: 227 us -> 227 us (level)
  no operation moved by 1% of the time
where the time goes in v2:
time: 227 us; the launch traced here: 224 us
  waiting for transfers between devices  105 us (46%)
  starting transfers between devices  82 us (36%)
  Pallas kernels  16 us (7%)
  other arithmetic  11.8 us (5%)
  local copies, waits for them, and re-layouts  6.26 us (3%)
    ppermute x1, waiting for transfers between devices, on_device(): beside = lax.ppermute(grad_kv, 'xl', swap)  45 us
    all_to_all x1, waiting for transfers between devices, on_device(): lax.all_to_all(jnp.broadcast_to(activations[None], (n_ten, own_rows, widt...  20.7 us
    ppermute x7, starting transfers between devices, on_device(): own = own + lax.ppermute(low(part[k]), 'z', shift).astype(jnp.float32)  16.3 us
    ppermute x7, starting transfers between devices, on_device(): grad_w = grad_w + lax.ppermute(x, 'z', shift).astype(jnp.float32)  15.9 us
    ppermute x3, waiting for transfers between devices, on_device(): a = lax.ppermute(a, 'z', up)  12 us
    all_to_all x1, starting transfers between devices, on_device(): part_1 = lax.all_to_all(add(near_1, far_1), 'z', 0, 0)  11.8 us
    pallas_call x1, Pallas kernels, attend(): pl.pallas_call(functools.partial(attention_kernel, len(blocks)), name='at...  10.7 us
    ppermute x3, starting transfers between devices, on_device(): a = lax.ppermute(a, 'z', up)  7.59 us
  transfers between devices with their start and end apart: 41, of which 22 were waited for; matrix products, arithmetic and copies ran while one was open for 6% of the time, Pallas kernels for 1%

profile of v2, /device:TPU:32, one launch (start us, length us, event | category | flops | bytes accessed | tf_op | source)
XLA Modules:
  0.0 223.9 jit_solution(10201590874137721020)
XLA Ops:
  0.6 2.4 %broadcast_in_dim.12 = bf16[8,24,5120]{2,1,0:T(8,128)(2,1)} broadcast(bf16[24,5120]{1,0:T(8,128)(2,1)} %param.9), dimensions={1,2} | broadcast | bytes 2211840 | tf_op jit(solution)/shard_map/broadcast_in_dim | solution.py:336
  3.1 7.1 %all-to-all-start = ((bf16[8,24,5120]{2,1,0:T(8,128)(2,1)}), bf16[8,24,5120]{2,1,0:T(8,128)(2,1)}, u32[]{:S(2)}, u32[]{:S(2)}) async-start(bf16[8,24,5120]{2,1,0:T(8,128)(2,1)} %broadcast_in_dim.12), calls=%async_computation | async-start | bytes 3932160 | tf_op jit(solution)/shard_map/all_to_all | solution.py:335
  10.3 0.6 convert_reduce_fusion
  12.6 2.0 pad_maximum_fusion.w_ref
  14.6 20.7 %all-to-all-done = bf16[8,24,5120]{2,1,0:T(8,128)(2,1)} async-done(((bf16[8,24,5120]{2,1,0:T(8,128)(2,1)}), bf16[8,24,5120]{2,1,0:T(8,128)(2,1)}, u32[]{:S(2)}, u32[]{:S(2)}) %all-to-all-start) | async-done | bytes 1966112 | tf_op jit(solution)/shard_map/all_to_all | solution.py:335
  35.3 2.2 constant_dynamic-update-slice_fusion.5
  37.5 0.7 collective-permute-start
  38.2 4.0 %collective-permute-done = bf16[192,256]{1,0:T(8,128)(2,1)S(1)} collective-permute-done((bf16[192,256]{1,0:T(8,128)(2,1)S(1)}, bf16[192,256]{1,0:T(8,128)(2,1)S(1)}, u32[]{:S(2)}, u32[]{:S(2)}) %collective-permute-start) | collective-permute-done | bytes 98336 | tf_op jit(solution)/shard_map/ppermute | solution.py:341
  42.2 2.0 collective-permute-start.1
  44.4 3.6 %collective-permute-done.1 = bf16[2,192,256]{2,1,0:T(8,128)(2,1)S(1)} collective-permute-done((bf16[2,192,256]{2,1,0:T(8,128)(2,1)S(1)}, bf16[2,192,256]{2,1,0:T(8,128)(2,1)S(1)}, u32[]{:S(2)}, u32[]{:S(2)}) %collective-permute-start.1) | collective-permute-done | bytes 196640 | tf_op jit(solution)/shard_map/ppermute | solution.py:346
  48.0 2.3 %collective-permute-start.3 = (bf16[2,192,256]{2,1,0:T(8,128)(2,1)S(1)}, bf16[2,192,256]{2,1,0:T(8,128)(2,1)S(1)}, u32[]{:S(2)}, u32[]{:S(2)}) collective-permute-start(bf16[2,192,256]{2,1,0:T(8,128)(2,1)S(1)} %collective-permute-done.1), channel_id=1, source_target_pairs={{0,32},{32,64},{64,96},{96,128},{128,160},{160,192},{192,224},{224... | collective-permute-start | bytes 589832 | tf_op jit(solution)/shard_map/ppermute | solution.py:346
  50.3 1.7 collective-permute-start.4
  52.0 3.6 %collective-permute-done.3 = bf16[2,192,256]{2,1,0:T(8,128)(2,1)S(1)} collective-permute-done((bf16[2,192,256]{2,1,0:T(8,128)(2,1)S(1)}, bf16[2,192,256]{2,1,0:T(8,128)(2,1)S(1)}, u32[]{:S(2)}, u32[]{:S(2)}) %collective-permute-start.3) | collective-permute-done | bytes 196640 | tf_op jit(solution)/shard_map/ppermute | solution.py:346
  55.6 1.0 collective-permute-done.4
  56.7 3.3 %collective-permute-start.5 = (bf16[2,192,256]{2,1,0:T(8,128)(2,1)S(1)}, bf16[2,192,256]{2,1,0:T(8,128)(2,1)S(1)}, u32[]{:S(2)}, u32[]{:S(2)}) collective-permute-start(bf16[2,192,256]{2,1,0:T(8,128)(2,1)S(1)} %collective-permute-done.3), channel_id=1, source_target_pairs={{0,32},{32,64},{64,96},{96,128},{128,160},{160,192},{192,224},{224... | collective-permute-start | bytes 589832 | tf_op jit(solution)/shard_map/ppermute | solution.py:346
  60.0 4.7 %collective-permute-done.5 = bf16[2,192,256]{2,1,0:T(8,128)(2,1)S(1)} collective-permute-done((bf16[2,192,256]{2,1,0:T(8,128)(2,1)S(1)}, bf16[2,192,256]{2,1,0:T(8,128)(2,1)S(1)}, u32[]{:S(2)}, u32[]{:S(2)}) %collective-permute-start.5) | collective-permute-done | bytes 196640 | tf_op jit(solution)/shard_map/ppermute | solution.py:346
  64.8 3.2 %collective-permute-start.7 = (bf16[1,192,256]{2,1,0:T(8,128)(2,1)S(1)}, bf16[1,192,256]{2,1,0:T(8,128)(2,1)S(1)}, u32[]{:S(2)}, u32[]{:S(2)}) collective-permute-start(bf16[1,192,256]{2,1,0:T(8,128)(2,1)S(1)} %slice.65), channel_id=1, source_target_pairs={{0,32},{32,64},{64,96},{96,128},{128,160},{160,192},{192,224},{224... | collective-permute-start | bytes 294920 | tf_op jit(solution)/shard_map/ppermute | solution.py:349
  68.7 2.0 collective-permute-done.7
  70.7 2.5 %collective-permute-done.8 = bf16[1,192,256]{2,1,0:T(8,128)(2,1)S(1)} collective-permute-done((bf16[1,192,256]{2,1,0:T(8,128)(2,1)S(1)}, bf16[1,192,256]{2,1,0:T(8,128)(2,1)S(1)}, u32[]{:S(2)}, u32[]{:S(2)}) %collective-permute-start.8) | collective-permute-done | bytes 98336 | tf_op jit(solution)/shard_map/ppermute | solution.py:350
  73.5 1.4 collective-permute-done.11.refs_5_
  75.0 10.7 %attention.1 = (bf16[192,640]{1,0:T(8,128)(2,1)}, bf16[192,640]{1,0:T(8,128)(2,1)}, bf16[16,96,256]{2,1,0:T(8,128)(2,1)S(1)}, bf16[8,96,256]{2,1,0:T(8,128)(2,1)...) custom-call(s32[136]{0:T(256)S(1)} %pad_add_fusion.2.table_ref, ...), custom_call_target="tpu_custom_call" | custom-call | tf_op jit(solution)/shard_map/attention/pallas_call | solution.py:161
  85.7 3.5 %collective-permute-start.13 = (bf16[8,96,256]{2,1,0:T(8,128)(2,1)S(1)}, bf16[8,96,256]{2,1,0:T(8,128)(2,1)S(1)}, u32[]{:S(2)}, u32[]{:S(2)}) collective-permute-start(bf16[8,96,256]{2,1,0:T(8,128)(2,1)S(1)} %get-tuple-element.38), channel_id=1, source_target_pairs={{0,8},{8,0},{1,9},{9,1},{2,10},{10,2},{3,11},{11,3},{4,12},{12,4},... | collective-permute-start | bytes 1179656 | tf_op jit(solution)/shard_map/ppermute | solution.py:366
  89.7 0.8 collective-permute-done.13
  90.5 0.9 add_convert_fusion.1
  91.4 3.0 %collective-permute-start.14 = (bf16[8,96,256]{2,1,0:T(8,128)(2,1)}, bf16[8,96,256]{2,1,0:T(8,128)(2,1)}, u32[]{:S(2)}, u32[]{:S(2)}) collective-permute-start(bf16[8,96,256]{2,1,0:T(8,128)(2,1)} %add_convert_fusion.1), channel_id=1, source_target_pairs={{0,16},{16,0},{1,17},{17,1},{2,18},{18,2},{3,19},{19,3},{4,20},{20... | collective-permute-start | bytes 1179656 | tf_op jit(solution)/shard_map/ppermute | solution.py:369
  94.4 0.8 add_convert_fusion
  95.3 11.8 %all-to-all-start.1 = ((bf16[8,96,256]{2,1,0:T(8,128)(2,1)}), bf16[8,96,256]{2,1,0:T(8,128)(2,1)}, u32[]{:S(2)}, u32[]{:S(2)}) async-start(bf16[8,96,256]{2,1,0:T(8,128)(2,1)} %add_convert_fusion), calls=%async_computation.1 | async-start | bytes 786432 | tf_op jit(solution)/shard_map/all_to_all | solution.py:370
  107.1 1.3 convert_add_fusion
  108.4 2.4 %fusion.21 = (bf16[8,2,96,256]{3,2,0,1:T(8,128)(2,1)S(1)}, f32[8,2,96,256]{3,2,0,1:T(8,128)}) fusion(bf16[8,1,96,256]{3,2,0,1:T(8,128)(2,1)} %bitcast.8, f32[8,2,96,256]{3,2,1,0:T(8,128)S(1)} %bitcast.84), kind=kLoop, calls=%fused_computation.77 | loop fusion | flops 1179648 | bytes 4325376 | tf_op jit(solution)/shard_map/convert.13
  110.8 0.7 slice_bitcast_fusion.7
  111.5 4.5 %collective-permute-start.15 = (bf16[2,96,256]{2,1,0:T(8,128)(2,1)S(1)}, bf16[2,96,256]{2,1,0:T(8,128)(2,1)S(1)}, u32[]{:S(2)}, u32[]{:S(2)}) collective-permute-start(bf16[2,96,256]{2,1,0:T(8,128)(2,1)S(1)} %get-tuple-element.60), channel_id=1, source_target_pairs={{0,128},{32,160},{64,192},{96,224},{128,0},{160,32},{192,64},{224,... | collective-permute-start | bytes 294920 | tf_op jit(solution)/shard_map/ppermute | solution.py:377
  116.0 1.5 collective-permute-start.16
  117.5 3.6 %collective-permute-start.17 = (bf16[2,96,256]{2,1,0:T(8,128)(2,1)}, bf16[2,96,256]{2,1,0:T(8,128)(2,1)S(1)}, u32[]{:S(2)}, u32[]{:S(2)}) collective-permute-start(bf16[2,96,256]{2,1,0:T(8,128)(2,1)} %get-tuple-element.63), channel_id=1, source_target_pairs={{0,96},{32,128},{64,160},{96,192},{128,224},{160,0},{192,32},{224,... | collective-permute-start | bytes 294920 | tf_op jit(solution)/shard_map/ppermute | solution.py:377
  121.0 2.4 %collective-permute-start.18 = (bf16[2,96,256]{2,1,0:T(8,128)(2,1)S(1)}, bf16[2,96,256]{2,1,0:T(8,128)(2,1)S(1)}, u32[]{:S(2)}, u32[]{:S(2)}) collective-permute-start(bf16[2,96,256]{2,1,0:T(8,128)(2,1)S(1)} %get-tuple-element.62), channel_id=1, source_target_pairs={{0,192},{32,224},{64,0},{96,32},{128,64},{160,96},{192,128},{224,1... | collective-permute-start | bytes 294920 | tf_op jit(solution)/shard_map/ppermute | solution.py:377
  123.4 2.4 %collective-permute-start.19 = (bf16[2,96,256]{2,1,0:T(8,128)(2,1)S(1)}, bf16[2,96,256]{2,1,0:T(8,128)(2,1)S(1)}, u32[]{:S(2)}, u32[]{:S(2)}) collective-permute-start(bf16[2,96,256]{2,1,0:T(8,128)(2,1)S(1)} %get-tuple-element.61), channel_id=1, source_target_pairs={{0,64},{32,96},{64,128},{96,160},{128,192},{160,224},{192,0},{224,... | collective-permute-start | bytes 294920 | tf_op jit(solution)/shard_map/ppermute | solution.py:377
  125.8 2.1 collective-permute-start.20
  127.8 3.0 %collective-permute-done.16 = bf16[2,96,256]{2,1,0:T(8,128)(2,1)S(1)} collective-permute-done((bf16[2,96,256]{2,1,0:T(8,128)(2,1)S(1)}, bf16[2,96,256]{2,1,0:T(8,128)(2,1)S(1)}, u32[]{:S(2)}, u32[]{:S(2)}) %collective-permute-start.16) | collective-permute-done | bytes 98336 | tf_op jit(solution)/shard_map/ppermute | solution.py:377
  130.8 1.7 reduce_sum.32
  132.5 1.8 collective-permute-start.23
  134.3 1.5 collective-permute-done.18
  135.8 1.7 collective-permute-done.20
  137.7 1.1 fusion.8
  138.9 1.0 grad_rows.1
  139.9 1.3 copy-done
  141.1 5.4 %all-to-all-start.2 = ((bf16[8,24,5120]{2,1,0:T(8,128)(2,1)}), bf16[8,24,5120]{2,1,0:T(8,128)(2,1)S(1)}, u32[]{:S(2)}, u32[]{:S(2)}) async-start(bf16[8,24,5120]{2,1,0:T(8,128)(2,1)} %bitcast.79), calls=%async_computation.2 | async-start | bytes 3932160 | tf_op jit(solution)/shard_map/all_to_all | solution.py:387
  146.6 2.5 %strips.1 = (bf16[8,160,192]{2,1,0:T(8,128)(2,1)S(1)}, bf16[8,160,192]{2,1,0:T(8,128)(2,1)S(1)}, bf16[8,160,192]{2,1,0:T(8,128)(2,1)S(1)}, bf16[8,160,192]{2,1,0:T(8,128)(2,1)S(1)}) custom-call(s32[4]{0:T(128)S(1)} %pad_add_fusion.3.at_ref, bf16[192,5120]{1,0:T(8,128)(2,1)} %bitcast.rows_ref), custom_call_target="tpu_custom_call" | custom-call | tf_op jit(solution)/shard_map/strips/pallas_call | solution.py:193
  150.0 1.3 collective-permute-done.26
  151.7 1.6 collective-permute-start.29
  153.3 45.0 %collective-permute-done.29.refs_6_ = bf16[192,256]{1,0:T(8,128)(2,1)S(1)} collective-permute-done((bf16[192,256]{1,0:T(8,128)(2,1)S(1)}, bf16[192,256]{1,0:T(8,128)(2,1)S(1)}, u32[]{:S(2)}, u32[]{:S(2)}) %collective-permute-start.29) | collective-permute-done | bytes 98336 | tf_op jit(solution)/shard_map/ppermute | solution.py:383
  198.3 1.3 collective-permute-done.30.refs_7_
  199.6 0.8 grad_w.1
  200.4 3.3 %collective-permute-start.31 = (bf16[160,256]{1,0:T(8,128)(2,1)S(1)}, bf16[160,256]{1,0:T(8,128)(2,1)S(1)}, u32[]{:S(2)}, u32[]{:S(2)}) collective-permute-start(bf16[160,256]{1,0:T(8,128)(2,1)S(1)} %get-tuple-element.46), channel_id=1, source_target_pairs={{0,128},{32,160},{64,192},{96,224},{128,0},{160,32},{192,64},{224,... | collective-permute-start | bytes 245768 | tf_op jit(solution)/shard_map/ppermute | solution.py:393
  203.7 2.9 %collective-permute-start.32 = (bf16[160,256]{1,0:T(8,128)(2,1)S(1)}, bf16[160,256]{1,0:T(8,128)(2,1)S(1)}, u32[]{:S(2)}, u32[]{:S(2)}) collective-permute-start(bf16[160,256]{1,0:T(8,128)(2,1)S(1)} %get-tuple-element.47), channel_id=1, source_target_pairs={{0,96},{32,128},{64,160},{96,192},{128,224},{160,0},{192,32},{224,... | collective-permute-start | bytes 245768 | tf_op jit(solution)/shard_map/ppermute | solution.py:393
  206.6 2.2 collective-permute-start.33
  208.7 1.6 collective-permute-start.34
  210.3 2.5 %collective-permute-start.35 = (bf16[160,256]{1,0:T(8,128)(2,1)S(1)}, bf16[160,256]{1,0:T(8,128)(2,1)S(1)}, u32[]{:S(2)}, u32[]{:S(2)}) collective-permute-start(bf16[160,256]{1,0:T(8,128)(2,1)S(1)} %get-tuple-element.50), channel_id=1, source_target_pairs={{0,192},{32,224},{64,0},{96,32},{128,64},{160,96},{192,128},{224,1... | collective-permute-start | bytes 245768 | tf_op jit(solution)/shard_map/ppermute | solution.py:393
  212.9 2.8 %collective-permute-start.36 = (bf16[160,256]{1,0:T(8,128)(2,1)S(1)}, bf16[160,256]{1,0:T(8,128)(2,1)S(1)}, u32[]{:S(2)}, u32[]{:S(2)}) collective-permute-start(bf16[160,256]{1,0:T(8,128)(2,1)S(1)} %get-tuple-element.51), channel_id=1, source_target_pairs={{0,32},{32,64},{64,96},{96,128},{128,160},{160,192},{192,224},{224... | collective-permute-start | bytes 245768 | tf_op jit(solution)/shard_map/ppermute | solution.py:393
  215.7 2.0 collective-permute-done.32
  217.7 0.6 collective-permute-start.37
  218.4 1.8 collective-permute-done.34
  220.2 0.6 collective-permute-done.36
  220.7 1.5 collective-permute-done.37
  222.3 0.7 fusion.24
  223.0 0.9 total.1
  (97 shorter events, 5.2 us)
Async XLA Ops:
  3.1 7.1 %copy-start.6 = (s32[64]{0:T(128)S(1)}, s32[64]{0:T(128)}, u32[]{:S(2)}) copy-start(s32[64]{0:T(128)} %param.14) | copy-start | bytes 772
  3.1 7.2 %copy-start.3 = (s32[6144]{0:T(1024)S(1)}, s32[6144]{0:T(1024)}, u32[]{:S(2)}) copy-start(s32[6144]{0:T(1024)} %param.15) | copy-start | bytes 73732
  3.1 8.3 %copy-start.4 = (s32[16]{0:T(128)S(1)}, s32[16]{0:T(128)}, u32[]{:S(2)}) copy-start(s32[16]{0:T(128)} %constant.106.clone) | copy-start | bytes 196
  3.1 8.3 %copy-start.5 = (s32[16]{0:T(128)S(1)}, s32[16]{0:T(128)}, u32[]{:S(2)}) copy-start(s32[16]{0:T(128)} %constant.116) | copy-start | bytes 196
  3.1 32.2 %all-to-all-start = ((bf16[8,24,5120]{2,1,0:T(8,128)(2,1)}), bf16[8,24,5120]{2,1,0:T(8,128)(2,1)}, u32[]{:S(2)}, u32[]{:S(2)}) async-start(bf16[8,24,5120]{2,1,0:T(8,128)(2,1)} %broadcast_in_dim.12), calls=%async_computation | async-start | bytes 3932160 | tf_op jit(solution)/shard_map/all_to_all | solution.py:335
  37.5 37.5 %copy-start.1 = (bf16[192,640]{1,0:T(8,128)(2,1)S(1)}, bf16[192,640]{1,0:T(8,128)(2,1)}, u32[]{:S(2)}) copy-start(bf16[192,640]{1,0:T(8,128)(2,1)} %q_ref.1) | copy-start | bytes 737284
  37.5 37.5 %copy-start.2 = (bf16[192,640]{1,0:T(8,128)(2,1)S(1)}, bf16[192,640]{1,0:T(8,128)(2,1)}, u32[]{:S(2)}) copy-start(bf16[192,640]{1,0:T(8,128)(2,1)} %g_ref.1) | copy-start | bytes 737284
  37.5 4.7 %collective-permute-start = (bf16[192,256]{1,0:T(8,128)(2,1)S(1)}, bf16[192,256]{1,0:T(8,128)(2,1)S(1)}, u32[]{:S(2)}, u32[]{:S(2)}) collective-permute-start(bf16[192,256]{1,0:T(8,128)(2,1)S(1)} %get-tuple-element.72), channel_id=1, source_target_pairs={{0,16},{16,0},{1,17},{17,1},{2,18},{18,2},{3,19},{19,3},{4,20},{20... | collective-permute-start | bytes 294920 | tf_op jit(solution)/shard_map/ppermute | solution.py:341
  42.2 5.7 %collective-permute-start.1 = (bf16[2,192,256]{2,1,0:T(8,128)(2,1)S(1)}, bf16[2,192,256]{2,1,0:T(8,128)(2,1)S(1)}, u32[]{:S(2)}, u32[]{:S(2)}) collective-permute-start(bf16[2,192,256]{2,1,0:T(8,128)(2,1)S(1)} %pad_maximum_fusion.1), channel_id=1, source_target_pairs={{0,32},{32,64},{64,96},{96,128},{128,160},{160,192},{192,224},{224... | collective-permute-start | bytes 589832 | tf_op jit(solution)/shard_map/ppermute | solution.py:346
  44.2 6.0 %collective-permute-start.2 = (bf16[2,192,256]{2,1,0:T(8,128)(2,1)S(1)}, bf16[2,192,256]{2,1,0:T(8,128)(2,1)S(1)}, u32[]{:S(2)}, u32[]{:S(2)}) collective-permute-start(bf16[2,192,256]{2,1,0:T(8,128)(2,1)S(1)} %pad_maximum_fusion.1), channel_id=1, source_target_pairs={{0,224},{32,0},{64,32},{96,64},{128,96},{160,128},{192,160},{224,1... | collective-permute-start | bytes 589832 | tf_op jit(solution)/shard_map/ppermute | solution.py:347
  48.0 7.6 %collective-permute-start.3 = (bf16[2,192,256]{2,1,0:T(8,128)(2,1)S(1)}, bf16[2,192,256]{2,1,0:T(8,128)(2,1)S(1)}, u32[]{:S(2)}, u32[]{:S(2)}) collective-permute-start(bf16[2,192,256]{2,1,0:T(8,128)(2,1)S(1)} %collective-permute-done.1), channel_id=1, source_target_pairs={{0,32},{32,64},{64,96},{96,128},{128,160},{160,192},{192,224},{224... | collective-permute-start | bytes 589832 | tf_op jit(solution)/shard_map/ppermute | solution.py:346
  50.3 6.3 %collective-permute-start.4 = (bf16[2,192,256]{2,1,0:T(8,128)(2,1)S(1)}, bf16[2,192,256]{2,1,0:T(8,128)(2,1)S(1)}, u32[]{:S(2)}, u32[]{:S(2)}) collective-permute-start(bf16[2,192,256]{2,1,0:T(8,128)(2,1)S(1)} %collective-permute-done.2), channel_id=1, source_target_pairs={{0,224},{32,0},{64,32},{96,64},{128,96},{160,128},{192,160},{224,1... | collective-permute-start | bytes 589832 | tf_op jit(solution)/shard_map/ppermute | solution.py:347
  56.6 18.4 %collective-permute-start.9 = (bf16[10,192,256]{2,1,0:T(8,128)(2,1)S(1)}, bf16[10,192,256]{2,1,0:T(8,128)(2,1)S(1)}, u32[]{:S(2)}, u32[]{:S(2)}) collective-permute-start(bf16[10,192,256]{2,1,0:T(8,128)(2,1)S(1)} %constant_dynamic-update-slice_fusion.refs_0_), channel_id=1, source_target_pairs={{0,8},{8,0},{1,9},{9,1},{2,10},{10,2},{3,11},{11,3},{4,12},{12,4},... | collective-permute-start | bytes 2949128 | tf_op jit(solution)/shard_map/ppermute | solution.py:354
  56.7 8.1 %collective-permute-start.5 = (bf16[2,192,256]{2,1,0:T(8,128)(2,1)S(1)}, bf16[2,192,256]{2,1,0:T(8,128)(2,1)S(1)}, u32[]{:S(2)}, u32[]{:S(2)}) collective-permute-start(bf16[2,192,256]{2,1,0:T(8,128)(2,1)S(1)} %collective-permute-done.3), channel_id=1, source_target_pairs={{0,32},{32,64},{64,96},{96,128},{128,160},{160,192},{192,224},{224... | collective-permute-start | bytes 589832 | tf_op jit(solution)/shard_map/ppermute | solution.py:346
  60.0 8.4 %collective-permute-start.6 = (bf16[2,192,256]{2,1,0:T(8,128)(2,1)S(1)}, bf16[2,192,256]{2,1,0:T(8,128)(2,1)S(1)}, u32[]{:S(2)}, u32[]{:S(2)}) collective-permute-start(bf16[2,192,256]{2,1,0:T(8,128)(2,1)S(1)} %collective-permute-done.4), channel_id=1, source_target_pairs={{0,224},{32,0},{64,32},{96,64},{128,96},{160,128},{192,160},{224,1... | collective-permute-start | bytes 589832 | tf_op jit(solution)/shard_map/ppermute | solution.py:347
  64.8 5.9 %collective-permute-start.7 = (bf16[1,192,256]{2,1,0:T(8,128)(2,1)S(1)}, bf16[1,192,256]{2,1,0:T(8,128)(2,1)S(1)}, u32[]{:S(2)}, u32[]{:S(2)}) collective-permute-start(bf16[1,192,256]{2,1,0:T(8,128)(2,1)S(1)} %slice.65), channel_id=1, source_target_pairs={{0,32},{32,64},{64,96},{96,128},{128,160},{160,192},{192,224},{224... | collective-permute-start | bytes 294920 | tf_op jit(solution)/shard_map/ppermute | solution.py:349
  68.5 4.8 %collective-permute-start.8 = (bf16[1,192,256]{2,1,0:T(8,128)(2,1)S(1)}, bf16[1,192,256]{2,1,0:T(8,128)(2,1)S(1)}, u32[]{:S(2)}, u32[]{:S(2)}) collective-permute-start(bf16[1,192,256]{2,1,0:T(8,128)(2,1)S(1)} %slice.66), channel_id=1, source_target_pairs={{0,224},{32,0},{64,32},{96,64},{128,96},{160,128},{192,160},{224,1... | collective-permute-start | bytes 294920 | tf_op jit(solution)/shard_map/ppermute | solution.py:350
  68.6 6.4 %collective-permute-start.10 = (bf16[4,192,256]{2,1,0:T(8,128)(2,1)S(1)}, bf16[4,192,256]{2,1,0:T(8,128)(2,1)S(1)}, u32[]{:S(2)}, u32[]{:S(2)}) collective-permute-start(bf16[4,192,256]{2,1,0:T(8,128)(2,1)S(1)} %constant_dynamic-update-slice_fusion.6.refs_1_), channel_id=1, source_target_pairs={{0,8},{8,0},{1,9},{9,1},{2,10},{10,2},{3,11},{11,3},{4,12},{12,4},... | collective-permute-start | bytes 1179656 | tf_op jit(solution)/shard_map/ppermute | solution.py:354
  73.3 1.7 collective-permute-start.11
  85.7 4.9 %collective-permute-start.13 = (bf16[8,96,256]{2,1,0:T(8,128)(2,1)S(1)}, bf16[8,96,256]{2,1,0:T(8,128)(2,1)S(1)}, u32[]{:S(2)}, u32[]{:S(2)}) collective-permute-start(bf16[8,96,256]{2,1,0:T(8,128)(2,1)S(1)} %get-tuple-element.38), channel_id=1, source_target_pairs={{0,8},{8,0},{1,9},{9,1},{2,10},{10,2},{3,11},{11,3},{4,12},{12,4},... | collective-permute-start | bytes 1179656 | tf_op jit(solution)/shard_map/ppermute | solution.py:366
  89.2 17.9 %collective-permute-start.12 = (bf16[16,96,256]{2,1,0:T(8,128)(2,1)}, bf16[16,96,256]{2,1,0:T(8,128)(2,1)}, u32[]{:S(2)}, u32[]{:S(2)}) collective-permute-start(bf16[16,96,256]{2,1,0:T(8,128)(2,1)} %get-tuple-element.36), channel_id=1, source_target_pairs={{0,8},{8,0},{1,9},{9,1},{2,10},{10,2},{3,11},{11,3},{4,12},{12,4},... | collective-permute-start | bytes 2359304 | tf_op jit(solution)/shard_map/ppermute | solution.py:368
  89.2 5.2 %collective-permute-start.22 = (bf16[8,96,256]{2,1,0:T(8,128)(2,1)S(1)}, bf16[8,96,256]{2,1,0:T(8,128)(2,1)S(1)}, u32[]{:S(2)}, u32[]{:S(2)}) collective-permute-start(bf16[8,96,256]{2,1,0:T(8,128)(2,1)S(1)} %get-tuple-element.40), channel_id=1, source_target_pairs={{0,8},{8,0},{1,9},{9,1},{2,10},{10,2},{3,11},{11,3},{4,12},{12,4},... | collective-permute-start | bytes 1179656 | tf_op jit(solution)/shard_map/ppermute | solution.py:367
  91.4 17.0 %collective-permute-start.14 = (bf16[8,96,256]{2,1,0:T(8,128)(2,1)}, bf16[8,96,256]{2,1,0:T(8,128)(2,1)}, u32[]{:S(2)}, u32[]{:S(2)}) collective-permute-start(bf16[8,96,256]{2,1,0:T(8,128)(2,1)} %add_convert_fusion.1), channel_id=1, source_target_pairs={{0,16},{16,0},{1,17},{17,1},{2,18},{18,2},{3,19},{19,3},{4,20},{20... | collective-permute-start | bytes 1179656 | tf_op jit(solution)/shard_map/ppermute | solution.py:369
  95.3 35.6 %all-to-all-start.1 = ((bf16[8,96,256]{2,1,0:T(8,128)(2,1)}), bf16[8,96,256]{2,1,0:T(8,128)(2,1)}, u32[]{:S(2)}, u32[]{:S(2)}) async-start(bf16[8,96,256]{2,1,0:T(8,128)(2,1)} %add_convert_fusion), calls=%async_computation.1 | async-start | bytes 786432 | tf_op jit(solution)/shard_map/all_to_all | solution.py:370
  111.5 14.2 %collective-permute-start.15 = (bf16[2,96,256]{2,1,0:T(8,128)(2,1)S(1)}, bf16[2,96,256]{2,1,0:T(8,128)(2,1)S(1)}, u32[]{:S(2)}, u32[]{:S(2)}) collective-permute-start(bf16[2,96,256]{2,1,0:T(8,128)(2,1)S(1)} %get-tuple-element.60), channel_id=1, source_target_pairs={{0,128},{32,160},{64,192},{96,224},{128,0},{160,32},{192,64},{224,... | collective-permute-start | bytes 294920 | tf_op jit(solution)/shard_map/ppermute | solution.py:377
  116.0 14.8 %collective-permute-start.16 = (bf16[2,96,256]{2,1,0:T(8,128)(2,1)S(1)}, bf16[2,96,256]{2,1,0:T(8,128)(2,1)S(1)}, u32[]{:S(2)}, u32[]{:S(2)}) collective-permute-start(bf16[2,96,256]{2,1,0:T(8,128)(2,1)S(1)} %get-tuple-element.64), channel_id=1, source_target_pairs={{0,160},{32,192},{64,224},{96,0},{128,32},{160,64},{192,96},{224,1... | collective-permute-start | bytes 294920 | tf_op jit(solution)/shard_map/ppermute | solution.py:377
  117.5 15.1 %collective-permute-start.17 = (bf16[2,96,256]{2,1,0:T(8,128)(2,1)}, bf16[2,96,256]{2,1,0:T(8,128)(2,1)S(1)}, u32[]{:S(2)}, u32[]{:S(2)}) collective-permute-start(bf16[2,96,256]{2,1,0:T(8,128)(2,1)} %get-tuple-element.63), channel_id=1, source_target_pairs={{0,96},{32,128},{64,160},{96,192},{128,224},{160,0},{192,32},{224,... | collective-permute-start | bytes 294920 | tf_op jit(solution)/shard_map/ppermute | solution.py:377
  121.0 14.8 %collective-permute-start.18 = (bf16[2,96,256]{2,1,0:T(8,128)(2,1)S(1)}, bf16[2,96,256]{2,1,0:T(8,128)(2,1)S(1)}, u32[]{:S(2)}, u32[]{:S(2)}) collective-permute-start(bf16[2,96,256]{2,1,0:T(8,128)(2,1)S(1)} %get-tuple-element.62), channel_id=1, source_target_pairs={{0,192},{32,224},{64,0},{96,32},{128,64},{160,96},{192,128},{224,1... | collective-permute-start | bytes 294920 | tf_op jit(solution)/shard_map/ppermute | solution.py:377
  123.4 12.4 %collective-permute-start.19 = (bf16[2,96,256]{2,1,0:T(8,128)(2,1)S(1)}, bf16[2,96,256]{2,1,0:T(8,128)(2,1)S(1)}, u32[]{:S(2)}, u32[]{:S(2)}) collective-permute-start(bf16[2,96,256]{2,1,0:T(8,128)(2,1)S(1)} %get-tuple-element.61), channel_id=1, source_target_pairs={{0,64},{32,96},{64,128},{96,160},{128,192},{160,224},{192,0},{224,... | collective-permute-start | bytes 294920 | tf_op jit(solution)/shard_map/ppermute | solution.py:377
  125.8 11.7 %collective-permute-start.20 = (bf16[2,96,256]{2,1,0:T(8,128)(2,1)S(1)}, bf16[2,96,256]{2,1,0:T(8,128)(2,1)}, u32[]{:S(2)}, u32[]{:S(2)}) collective-permute-start(bf16[2,96,256]{2,1,0:T(8,128)(2,1)S(1)} %get-tuple-element.66), channel_id=1, source_target_pairs={{0,224},{32,0},{64,32},{96,64},{128,96},{160,128},{192,160},{224,1... | collective-permute-start | bytes 294920 | tf_op jit(solution)/shard_map/ppermute | solution.py:377
  130.8 6.9 %collective-permute-start.21 = (bf16[2,96,256]{2,1,0:T(8,128)(2,1)S(1)}, bf16[2,96,256]{2,1,0:T(8,128)(2,1)}, u32[]{:S(2)}, u32[]{:S(2)}) collective-permute-start(bf16[2,96,256]{2,1,0:T(8,128)(2,1)S(1)} %get-tuple-element.65), channel_id=1, source_target_pairs={{0,32},{32,64},{64,96},{96,128},{128,160},{160,192},{192,224},{224... | collective-permute-start | bytes 294920 | tf_op jit(solution)/shard_map/ppermute | solution.py:377
  132.5 5.2 %collective-permute-start.23 = (bf16[96,256]{1,0:T(8,128)(2,1)}, bf16[96,256]{1,0:T(8,128)(2,1)S(1)}, u32[]{:S(2)}, u32[]{:S(2)}) collective-permute-start(bf16[96,256]{1,0:T(8,128)(2,1)} %reduce_sum.32), channel_id=1, source_target_pairs={{0,16},{16,0},{1,17},{17,1},{2,18},{18,2},{3,19},{19,3},{4,20},{20... | collective-permute-start | bytes 147464 | tf_op jit(solution)/shard_map/ppermute | solution.py:379
  139.9 1.3 copy-start
  141.1 81.8 %all-to-all-start.2 = ((bf16[8,24,5120]{2,1,0:T(8,128)(2,1)}), bf16[8,24,5120]{2,1,0:T(8,128)(2,1)S(1)}, u32[]{:S(2)}, u32[]{:S(2)}) async-start(bf16[8,24,5120]{2,1,0:T(8,128)(2,1)} %bitcast.79), calls=%async_computation.2 | async-start | bytes 3932160 | tf_op jit(solution)/shard_map/all_to_all | solution.py:387
  149.1 2.2 collective-permute-start.26
  149.2 49.1 %collective-permute-start.24 = (bf16[8,160,192]{2,1,0:T(8,128)(2,1)S(1)}, bf16[8,160,192]{2,1,0:T(8,128)(2,1)S(1)}, u32[]{:S(2)}, u32[]{:S(2)}) collective-permute-start(bf16[8,160,192]{2,1,0:T(8,128)(2,1)S(1)} %get-tuple-element.42), channel_id=1, source_target_pairs={{0,8},{8,0},{1,9},{9,1},{2,10},{10,2},{3,11},{11,3},{4,12},{12,4},... | collective-permute-start | bytes 1474568 | tf_op jit(solution)/shard_map/ppermute | solution.py:359
  149.7 48.6 %collective-permute-start.25 = (bf16[8,160,192]{2,1,0:T(8,128)(2,1)S(1)}, bf16[8,160,192]{2,1,0:T(8,128)(2,1)S(1)}, u32[]{:S(2)}, u32[]{:S(2)}) collective-permute-start(bf16[8,160,192]{2,1,0:T(8,128)(2,1)S(1)} %get-tuple-element.43), channel_id=1, source_target_pairs={{0,16},{16,0},{1,17},{17,1},{2,18},{18,2},{3,19},{19,3},{4,20},{20... | collective-permute-start | bytes 1474568 | tf_op jit(solution)/shard_map/ppermute | solution.py:358
  151.3 47.0 %collective-permute-start.27 = (bf16[8,160,192]{2,1,0:T(8,128)(2,1)S(1)}, bf16[8,160,192]{2,1,0:T(8,128)(2,1)S(1)}, u32[]{:S(2)}, u32[]{:S(2)}) collective-permute-start(bf16[8,160,192]{2,1,0:T(8,128)(2,1)S(1)} %collective-permute-done.26), channel_id=1, source_target_pairs={{0,16},{16,0},{1,17},{17,1},{2,18},{18,2},{3,19},{19,3},{4,20},{20... | collective-permute-start | bytes 1474568 | tf_op jit(solution)/shard_map/ppermute | solution.py:360
  151.7 46.6 %collective-permute-start.29 = (bf16[192,256]{1,0:T(8,128)(2,1)S(1)}, bf16[192,256]{1,0:T(8,128)(2,1)S(1)}, u32[]{:S(2)}, u32[]{:S(2)}) collective-permute-start(bf16[192,256]{1,0:T(8,128)(2,1)S(1)} %bitcast.81), channel_id=1, source_target_pairs={{0,16},{16,0},{1,17},{17,1},{2,18},{18,2},{3,19},{19,3},{4,20},{20... | collective-permute-start | bytes 294920 | tf_op jit(solution)/shard_map/ppermute | solution.py:383
  153.3 45.0 %collective-permute-start.28 = (bf16[192,256]{1,0:T(8,128)(2,1)S(1)}, bf16[192,256]{1,0:T(8,128)(2,1)S(1)}, u32[]{:S(2)}, u32[]{:S(2)}) collective-permute-start(bf16[192,256]{1,0:T(8,128)(2,1)S(1)} %bitcast.82), channel_id=1, source_target_pairs={{0,8},{8,0},{1,9},{9,1},{2,10},{10,2},{3,11},{11,3},{4,12},{12,4},... | collective-permute-start | bytes 294920 | tf_op jit(solution)/shard_map/ppermute | solution.py:384
  198.3 1.3 collective-permute-start.30
  200.4 12.4 %collective-permute-start.31 = (bf16[160,256]{1,0:T(8,128)(2,1)S(1)}, bf16[160,256]{1,0:T(8,128)(2,1)S(1)}, u32[]{:S(2)}, u32[]{:S(2)}) collective-permute-start(bf16[160,256]{1,0:T(8,128)(2,1)S(1)} %get-tuple-element.46), channel_id=1, source_target_pairs={{0,128},{32,160},{64,192},{96,224},{128,0},{160,32},{192,64},{224,... | collective-permute-start | bytes 245768 | tf_op jit(solution)/shard_map/ppermute | solution.py:393
  203.7 14.1 %collective-permute-start.32 = (bf16[160,256]{1,0:T(8,128)(2,1)S(1)}, bf16[160,256]{1,0:T(8,128)(2,1)S(1)}, u32[]{:S(2)}, u32[]{:S(2)}) collective-permute-start(bf16[160,256]{1,0:T(8,128)(2,1)S(1)} %get-tuple-element.47), channel_id=1, source_target_pairs={{0,96},{32,128},{64,160},{96,192},{128,224},{160,0},{192,32},{224,... | collective-permute-start | bytes 245768 | tf_op jit(solution)/shard_map/ppermute | solution.py:393
  206.6 11.8 %collective-permute-start.33 = (bf16[160,256]{1,0:T(8,128)(2,1)S(1)}, bf16[160,256]{1,0:T(8,128)(2,1)S(1)}, u32[]{:S(2)}, u32[]{:S(2)}) collective-permute-start(bf16[160,256]{1,0:T(8,128)(2,1)S(1)} %get-tuple-element.48), channel_id=1, source_target_pairs={{0,160},{32,192},{64,224},{96,0},{128,32},{160,64},{192,96},{224,1... | collective-permute-start | bytes 245768 | tf_op jit(solution)/shard_map/ppermute | solution.py:393
  208.7 11.4 %collective-permute-start.34 = (bf16[160,256]{1,0:T(8,128)(2,1)S(1)}, bf16[160,256]{1,0:T(8,128)(2,1)S(1)}, u32[]{:S(2)}, u32[]{:S(2)}) collective-permute-start(bf16[160,256]{1,0:T(8,128)(2,1)S(1)} %get-tuple-element.49), channel_id=1, source_target_pairs={{0,64},{32,96},{64,128},{96,160},{128,192},{160,224},{192,0},{224,... | collective-permute-start | bytes 245768 | tf_op jit(solution)/shard_map/ppermute | solution.py:393
  210.3 9.8 %collective-permute-start.35 = (bf16[160,256]{1,0:T(8,128)(2,1)S(1)}, bf16[160,256]{1,0:T(8,128)(2,1)S(1)}, u32[]{:S(2)}, u32[]{:S(2)}) collective-permute-start(bf16[160,256]{1,0:T(8,128)(2,1)S(1)} %get-tuple-element.50), channel_id=1, source_target_pairs={{0,192},{32,224},{64,0},{96,32},{128,64},{160,96},{192,128},{224,1... | collective-permute-start | bytes 245768 | tf_op jit(solution)/shard_map/ppermute | solution.py:393
  212.9 7.9 %collective-permute-start.36 = (bf16[160,256]{1,0:T(8,128)(2,1)S(1)}, bf16[160,256]{1,0:T(8,128)(2,1)S(1)}, u32[]{:S(2)}, u32[]{:S(2)}) collective-permute-start(bf16[160,256]{1,0:T(8,128)(2,1)S(1)} %get-tuple-element.51), channel_id=1, source_target_pairs={{0,32},{32,64},{64,96},{96,128},{128,160},{160,192},{192,224},{224... | collective-permute-start | bytes 245768 | tf_op jit(solution)/shard_map/ppermute | solution.py:393
  217.7 4.4 %collective-permute-start.37 = (bf16[160,256]{1,0:T(8,128)(2,1)S(1)}, bf16[160,256]{1,0:T(8,128)(2,1)S(1)}, u32[]{:S(2)}, u32[]{:S(2)}) collective-permute-start(bf16[160,256]{1,0:T(8,128)(2,1)S(1)} %get-tuple-element.52), channel_id=1, source_target_pairs={{0,224},{32,0},{64,32},{96,64},{128,96},{160,128},{192,160},{224,1... | collective-permute-start | bytes 245768 | tf_op jit(solution)/shard_map/ppermute | solution.py:393
